TPU v7x, 32 devices: a whole 2x2x4 slice. The times are simulated.
32 devices in a mesh: lon: 8 (over z, y), lat: 4 (over x, core).
Axes of the slice: x: 2, y: 2, z: 4, core: 2. Of those that a mesh axis runs over, the one named last changes fastest.
Arguments:
- crosswise_speed_units: float32 [8, 64, 2048], P(None, 'lat', 'lon'), may hold values from -6 to 6
- poleward_speed_units: float32 [8, 64, 2048], P(None, 'lat', 'lon'), may hold values from -6 to 6
- thermal_anomaly: float32 [8, 64, 2048], P(None, 'lat', 'lon'), may hold values from -6 to 6
- saltiness_anomaly: float32 [8, 64, 2048], P(None, 'lat', 'lon'), may hold values from -6 to 6
- freeboard_elevation: float32 [64, 2048], P('lat', 'lon'), may hold values from -6 to 6
- barotropic_zonal_flow: float32 [64, 2048], P('lat', 'lon'), may hold values from -6 to 6
- barotropic_meridional_flow: float32 [64, 2048], P('lat', 'lon'), may hold values from -6 to 6
- submerged_layer_tally: int32 [64, 2048], P('lat', 'lon'), may hold values from 0 to 8
- seam_partner_index: int32 [2048], P('lon'), may hold values from 0 to 2047, as said below
Outputs:
- zonal_speed_final: float32 [8, 64, 2048], P(None, 'lat', 'lon')
- poleward_speed_final: float32 [8, 64, 2048], P(None, 'lat', 'lon')
- thermal_final: float32 [8, 64, 2048], P(None, 'lat', 'lon')
- saltiness_final: float32 [8, 64, 2048], P(None, 'lat', 'lon')
- freeboard_final: float32 [64, 2048], P('lat', 'lon')
- barotropic_zonal_final: float32 [64, 2048], P('lat', 'lon')
- barotropic_meridional_final: float32 [64, 2048], P('lat', 'lon')
Inputs may be any that keep to these rules, and one draw needn't show every extreme that they name: seam_partner_index[seam_partner_index[c]] = c, and seam_partner_index[(c + 1) mod 2048] = (seam_partner_index[c] - 1) mod 2048 for every column c.
All inputs are finite; a program needn't handle non-finite values.
Results may differ from a plain program's by a relative error of at most 0.0003.
Values sent between devices are 32-bit elements; how exact they have to be, the bound alone decides.
No kernel may reach another device: no remote copies, remote signals or barrier semaphores. Data moves between devices by JAX's collectives and lax.ppermute only.
A program may use at most 128 MiB of HBM per device.

v0:
```python
import jax
import jax.numpy as jnp
from jax import lax
from jax.sharding import PartitionSpec as P

SUBSTEPS = 12


COURANT = 0.15
PRESSURE_GAIN = 0.1
CORIOLIS = 0.3
WAVE_MASS = 1.2
WAVE_MOMENTUM = 1.2
EPSILON = 1e-06


def extended_2(cells, sides, width, closed):
    for axis, dim in sides:
        count = lax.axis_size(axis)
        ends = count if closed else count - 1
        head = lax.slice_in_dim(cells, 0, width, axis=dim)
        tail = lax.slice_in_dim(cells, cells.shape[dim] - width, cells.shape[dim], axis=dim)
        cells = jnp.concatenate(
            [
                lax.ppermute(tail, axis, [(i, (i + 1) % count) for i in range(ends)]),
                cells,
                lax.ppermute(head, axis, [((i + 1) % count, i) for i in range(ends)]),
            ],
            axis=dim,
        )
    return cells


def weno_face(far_up, near_up, centre, near_down, far_down):
    poly_zero = (2.0 * far_up - 7.0 * near_up + 11.0 * centre) / 6.0
    poly_one = (-near_up + 5.0 * centre + 2.0 * near_down) / 6.0
    poly_two = (2.0 * centre + 5.0 * near_down - far_down) / 6.0
    smooth_zero = (
        13.0 / 12.0 * (far_up - 2.0 * near_up + centre) ** 2
        + 0.25 * (far_up - 4.0 * near_up + 3.0 * centre) ** 2
    )
    smooth_one = (
        13.0 / 12.0 * (near_up - 2.0 * centre + near_down) ** 2 + 0.25 * (near_up - near_down) ** 2
    )
    smooth_two = (
        13.0 / 12.0 * (centre - 2.0 * near_down + far_down) ** 2
        + 0.25 * (3.0 * centre - 4.0 * near_down + far_down) ** 2
    )
    weight_zero = 0.1 / (EPSILON + smooth_zero) ** 2
    weight_one = 0.6 / (EPSILON + smooth_one) ** 2
    weight_two = 0.3 / (EPSILON + smooth_two) ** 2
    return (weight_zero * poly_zero + weight_one * poly_one + weight_two * poly_two) / (
        weight_zero + weight_one + weight_two
    )


def face_fluxes(prognostic_bundle, velocity, wet_mask, along, length):

    def window(values, offset):
        return lax.slice_in_dim(values, offset, offset + length + 1, axis=along)

    face_speed = (
        0.5
        * (window(velocity, 2) + window(velocity, 3))
        * window(wet_mask, 2)
        * window(wet_mask, 3)
    )
    upwind = weno_face(
        window(prognostic_bundle, 0),
        window(prognostic_bundle, 1),
        window(prognostic_bundle, 2),
        window(prognostic_bundle, 3),
        window(prognostic_bundle, 4),
    )
    downwind = weno_face(
        window(prognostic_bundle, 5),
        window(prognostic_bundle, 4),
        window(prognostic_bundle, 3),
        window(prognostic_bundle, 2),
        window(prognostic_bundle, 1),
    )
    fluxes = COURANT * face_speed * jnp.where(face_speed >= 0.0, upwind, downwind)
    return (fluxes, face_speed)


def partner_fold(tops, parity, lead_offset, column_count, first_partner, northern, total_columns):
    facing = jnp.remainder(
        first_partner - lead_offset - lax.iota(jnp.int32, column_count), total_columns
    )
    picked = jnp.take(jnp.flip(tops, axis=1), facing, axis=2)
    return jnp.where(northern, parity * picked, 0.0)


def extend_deep(stacked_fields, parity, first_partner, northern, total_columns):
    channels, tile_rows, tile_cols = stacked_fields.shape
    east_west = extended_2(stacked_fields, (("lon", 2),), 3, True)
    north_south = extended_2(stacked_fields, (("lat", 1),), 3, False)
    tops = lax.all_gather(stacked_fields[:, tile_rows - 3 :, :], "lon", axis=2, tiled=True)
    ghosts = partner_fold(tops, parity, 0, tile_cols, first_partner, northern, total_columns)
    north_south = jnp.concatenate(
        [north_south[:, : tile_rows + 3], north_south[:, tile_rows + 3 :] + ghosts], axis=1
    )
    return (east_west, north_south)


def extend_wave(stacked_fields, margin, parity, first_partner, northern, total_columns):
    channels, tile_rows, tile_cols = stacked_fields.shape
    east_west = extended_2(stacked_fields, (("lon", 2),), margin, True)
    whole = extended_2(east_west, (("lat", 1),), margin, False)
    tops = lax.all_gather(stacked_fields[:, tile_rows - margin :, :], "lon", axis=2, tiled=True)
    ghosts = partner_fold(
        tops, parity, -margin, tile_cols + 2 * margin, first_partner, northern, total_columns
    )
    return jnp.concatenate(
        [whole[:, : tile_rows + margin], whole[:, tile_rows + margin :] + ghosts], axis=1
    )


def on_device(
    crosswise_speed_units,
    poleward_speed_units,
    thermal_anomaly,
    saltiness_anomaly,
    freeboard_elevation,
    barotropic_zonal_flow,
    barotropic_meridional_flow,
    submerged_layer_tally,
    seam_partner_index,
):
    levels, tile_rows, tile_cols = crosswise_speed_units.shape
    lat_size = lax.axis_size("lat")
    lon_size = lax.axis_size("lon")
    lat_index = lax.axis_index("lat")
    total_rows = tile_rows * lat_size
    total_columns = tile_cols * lon_size
    northern = lat_index == lat_size - 1
    first_partner = seam_partner_index[0]
    block_steps = 6
    margin = 2 * block_steps
    layer_total_real = submerged_layer_tally.astype(jnp.float32)
    stacked_fields = jnp.concatenate(
        [
            crosswise_speed_units,
            poleward_speed_units,
            thermal_anomaly,
            saltiness_anomaly,
            layer_total_real[None],
        ],
        axis=0,
    )
    parity = jnp.concatenate(
        [
            jnp.full((2 * levels, 1, 1), -1.0, jnp.float32),
            jnp.ones((2 * levels + 1, 1, 1), jnp.float32),
        ],
        axis=0,
    )
    east_west, north_south = extend_deep(
        stacked_fields, parity, first_partner, northern, total_columns
    )
    level_index = lax.broadcasted_iota(jnp.float32, (levels, 1, 1), 0)
    submerged_indicator = (level_index < layer_total_real[None]).astype(jnp.float32)
    wet_east = (level_index < east_west[4 * levels][None]).astype(jnp.float32)
    wet_north = (level_index < north_south[4 * levels][None]).astype(jnp.float32)
    fields_east = east_west[: 4 * levels].reshape(4, levels, tile_rows, tile_cols + 6)
    fields_north = north_south[: 4 * levels].reshape(4, levels, tile_rows + 6, tile_cols)
    flux_east, speed_east = face_fluxes(fields_east, fields_east[0:1], wet_east[None], 3, tile_cols)
    flux_north, speed_north = face_fluxes(
        fields_north, fields_north[1:2], wet_north[None], 2, tile_rows
    )
    prognostic_rate = -(flux_east[:, :, :, 1:] - flux_east[:, :, :, :-1]) - (
        flux_north[:, :, 1:, :] - flux_north[:, :, :-1, :]
    )
    spread = (
        speed_east[0, :, :, 1:]
        - speed_east[0, :, :, :-1]
        + (speed_north[0, :, 1:, :] - speed_north[0, :, :-1, :])
    )
    upward = -jnp.flip(jnp.cumsum(jnp.flip(spread, 0), axis=0), 0)
    prognostic_bundle = jnp.stack(
        [crosswise_speed_units, poleward_speed_units, thermal_anomaly, saltiness_anomaly], axis=0
    )
    interior = (
        COURANT * upward[None, 1:] * 0.5 * (prognostic_bundle[:, :-1] + prognostic_bundle[:, 1:])
    )
    boundary = jnp.zeros((4, 1, tile_rows, tile_cols), jnp.float32)
    vertical_flux = jnp.concatenate([boundary, interior, boundary], axis=1)
    prognostic_rate = prognostic_rate - (vertical_flux[:, :-1] - vertical_flux[:, 1:])
    density_east = 0.8 * fields_east[3] - 0.2 * fields_east[2]
    pressure_east = jnp.cumsum(density_east, axis=0) - 0.5 * density_east
    grad_east = 0.5 * (
        pressure_east[:, :, 4 : tile_cols + 4] - pressure_east[:, :, 2 : tile_cols + 2]
    )
    density_north = 0.8 * fields_north[3] - 0.2 * fields_north[2]
    pressure_north = jnp.cumsum(density_north, axis=0) - 0.5 * density_north
    grad_north = 0.5 * (
        pressure_north[:, 4 : tile_rows + 4, :] - pressure_north[:, 2 : tile_rows + 2, :]
    )
    own_rows = (lat_index * tile_rows + lax.iota(jnp.int32, tile_rows)).astype(jnp.float32)[:, None]
    coriolis = CORIOLIS * (2.0 * (own_rows + 0.5) / total_rows - 1.0)
    force_zonal = prognostic_rate[0] + coriolis * poleward_speed_units - PRESSURE_GAIN * grad_east
    force_merid = prognostic_rate[1] - coriolis * crosswise_speed_units - PRESSURE_GAIN * grad_north
    column = jnp.maximum(submerged_layer_tally, 1).astype(jnp.float32)
    mean_zonal = jnp.sum(submerged_indicator * force_zonal, axis=0) / column
    mean_merid = jnp.sum(submerged_indicator * force_merid, axis=0) / column
    static_parity = jnp.array([1.0, -1.0, -1.0], jnp.float32)[:, None, None]
    statics = extend_wave(
        jnp.stack([layer_total_real, mean_zonal, mean_merid], axis=0),
        margin,
        static_parity,
        first_partner,
        northern,
        total_columns,
    )
    thickness = statics[0] / levels
    wet_column = (statics[0] > 0.0).astype(jnp.float32)
    global_rows = lat_index * tile_rows - margin + lax.iota(jnp.int32, tile_rows + 2 * margin)
    mirrored = jnp.minimum(global_rows, 2 * total_rows - 1 - global_rows).astype(jnp.float32)[
        :, None
    ]
    coriolis_wide = CORIOLIS * (2.0 * (mirrored + 0.5) / total_rows - 1.0)

    def trim(values, keep):
        return values[
            margin - keep : margin + tile_rows + keep, margin - keep : margin + tile_cols + keep
        ]

    wave_parity = jnp.array([1.0, -1.0, -1.0], jnp.float32)[:, None, None]
    sea_level, zonal_flow, merid_flow = (
        freeboard_elevation,
        barotropic_zonal_flow,
        barotropic_meridional_flow,
    )
    for block in range(SUBSTEPS // block_steps):
        extended = extend_wave(
            jnp.stack([sea_level, zonal_flow, merid_flow], axis=0),
            margin,
            wave_parity,
            first_partner,
            northern,
            total_columns,
        )
        sea_level, zonal_flow, merid_flow = (extended[0], extended[1], extended[2])
        for inner_step in range(block_steps):
            outer = margin - 2 * inner_step
            keep = outer - 2
            thick = trim(thickness, outer)
            mass_east = thick * zonal_flow
            mass_north = thick * merid_flow
            spread_wave = 0.5 * (mass_east[1:-1, 2:] - mass_east[1:-1, :-2]) + 0.5 * (
                mass_north[2:, 1:-1] - mass_north[:-2, 1:-1]
            )
            next_level = trim(wet_column, outer - 1) * (
                sea_level[1:-1, 1:-1] - WAVE_MASS * spread_wave
            )
            rotation = coriolis_wide[margin - keep : margin + tile_rows + keep]
            wet_keep = trim(wet_column, keep)
            inner_zonal = zonal_flow[2:-2, 2:-2]
            inner_merid = merid_flow[2:-2, 2:-2]
            zonal_flow = wet_keep * (
                inner_zonal
                - WAVE_MOMENTUM * 0.5 * (next_level[1:-1, 2:] - next_level[1:-1, :-2])
                + (rotation * inner_merid + trim(statics[1], keep)) / SUBSTEPS
            )
            merid_flow = wet_keep * (
                inner_merid
                - WAVE_MOMENTUM * 0.5 * (next_level[2:, 1:-1] - next_level[:-2, 1:-1])
                + (-rotation * inner_zonal + trim(statics[2], keep)) / SUBSTEPS
            )
            sea_level = next_level[1:-1, 1:-1]
    zonal_speed_final = submerged_indicator * (
        crosswise_speed_units + force_zonal - mean_zonal + (zonal_flow - barotropic_zonal_flow)
    )
    poleward_speed_final = submerged_indicator * (
        poleward_speed_units + force_merid - mean_merid + (merid_flow - barotropic_meridional_flow)
    )
    thermal_final = submerged_indicator * (thermal_anomaly + prognostic_rate[2])
    saltiness_final = submerged_indicator * (saltiness_anomaly + prognostic_rate[3])
    return (
        zonal_speed_final,
        poleward_speed_final,
        thermal_final,
        saltiness_final,
        sea_level,
        zonal_flow,
        merid_flow,
    )


def solution(mesh):
    placed = (
        P(None, "lat", "lon"),
        P(None, "lat", "lon"),
        P(None, "lat", "lon"),
        P(None, "lat", "lon"),
        P("lat", "lon"),
        P("lat", "lon"),
        P("lat", "lon"),
        P("lat", "lon"),
        P("lon"),
    )
    return jax.shard_map(
        on_device,
        mesh=mesh,
        in_specs=placed,
        out_specs=(
            P(None, "lat", "lon"),
            P(None, "lat", "lon"),
            P(None, "lat", "lon"),
            P(None, "lat", "lon"),
            P("lat", "lon"),
            P("lat", "lon"),
            P("lat", "lon"),
        ),
        check_vma=False,
    )
```

profile of v0, /device:TPU:3, one launch (start us, length us, event | category | flops | bytes accessed | tf_op | source)
XLA Modules:
  0.0 296.0 jit_solution(17658706679827525291)
XLA Ops:
  6.2 3.2 %collective-permute-start.3 = (f32[33,3,256]{2,0,1:T(8,128)}, f32[33,3,256]{2,0,1:T(8,128)}, u32[]{:S(2)}, u32[]{:S(2)}) collective-permute-start(f32[33,3,256]{2,0,1:T(8,128)} %get-tuple-element.96), channel_id=1, source_target_pairs={{1,0},{2,1},{3,2},{5,4},{6,5},{7,6},{9,8},{10,9},{11,10},{13,12},{... | collective-permute-start | bytes 304136 | tf_op jit(solution)/shard_map/ppermute | solution.py:27
  9.5 1.3 collective-permute-start.2
  10.9 4.3 %collective-permute-start.1 = (f32[33,16,3]{2,1,0:T(8,128)S(1)}, f32[33,16,3]{2,1,0:T(8,128)S(1)}, u32[]{:S(2)}, u32[]{:S(2)}) collective-permute-start(f32[33,16,3]{2,1,0:T(8,128)S(1)} %get-tuple-element.104), channel_id=1, source_target_pairs={{4,0},{8,4},{12,8},{16,12},{20,16},{24,20},{28,24},{0,28},{5,1},{9... | collective-permute-start | bytes 19016 | tf_op jit(solution)/shard_map/ppermute | solution.py:27
  18.1 28.6 %all_gather.12 = f32[33,3,2048]{2,0,1:T(8,128)S(1)} all-gather(f32[33,3,256]{2,0,1:T(8,128)} %get-tuple-element.95), channel_id=1, replica_groups=mesh['lon'=8,'lat'=4] {'lon'}, dimensions={2}, use_global_device_ids=true | all-gather | bytes 912384 | tf_op jit(solution)/shard_map/all_gather | solution.py:98
  55.9 25.3 %all_gather.14 = f32[3,12,2048]{2,1,0:T(8,128)S(1)} all-gather(f32[3,12,256]{2,1,0:T(8,128)} %slice.1172), channel_id=1, replica_groups=mesh['lon'=8,'lat'=4] {'lon'}, dimensions={2}, use_global_device_ids=true | all-gather | bytes 331776 | tf_op jit(solution)/shard_map/all_gather | solution.py:110
  82.5 3.1 %copy.196 = f32[33,3,2048]{0,1,2:T(4,128)} copy(f32[33,3,2048]{2,0,1:T(8,128)S(1)} %all_gather.12) | data formatting | bytes 1622016 | tf_op jit(solution)/shard_map/all_gather | solution.py:98
  85.6 11.6 %rev.21 = f32[33,3,2048]{0,1,2:T(4,128)} reverse(f32[33,3,2048]{0,1,2:T(4,128)} %copy.196), dimensions={1} | reverse | bytes 1622016 | tf_op jit(solution)/shard_map/jit(_flip)/rev | solution.py:90
  97.2 3.2 %gather_fusion = f32[256,33,3]{1,2,0:T(4,128)S(1)} fusion(f32[33,3,2048]{0,1,2:T(4,128)} %rev.21, s32[1024]{0:T(1024)S(1)} %pad_clamp_fusion.1), kind=kCustom, calls=%fused_computation.3 | custom fusion | bytes 203776 | tf_op jit(solution)/shard_map/jit(_take)/gather | solution.py:90
  101.3 3.2 %copy.214 = f32[3,12,2048]{1,0,2:T(4,128)} copy(f32[3,12,2048]{2,1,0:T(8,128)S(1)} %all_gather.14) | data formatting | bytes 589824 | tf_op jit(solution)/shard_map/all_gather | solution.py:110
  104.4 12.0 %rev.25 = f32[3,12,2048]{1,0,2:T(4,128)} reverse(f32[3,12,2048]{1,0,2:T(4,128)} %copy.214), dimensions={1} | reverse | bytes 589824 | tf_op jit(solution)/shard_map/jit(_flip)/rev | solution.py:90
  116.4 4.1 %gather_fusion.2 = f32[280,3,12]{2,1,0:T(4,128)} fusion(f32[3,12,2048]{1,0,2:T(4,128)} %rev.25, s32[1024]{0:T(1024)S(1)} %pad_clamp_fusion), kind=kCustom, calls=%fused_computation.1.clone | custom fusion | bytes 81760 | tf_op jit(solution)/shard_map/jit(_take)/gather | solution.py:90
  122.0 15.5 %collective-permute-start.11 = (f32[3,12,280]{2,1,0:T(8,128)}, f32[3,12,280]{2,1,0:T(8,128)}, u32[]{:S(2)}, u32[]{:S(2)}) collective-permute-start(f32[3,12,280]{2,1,0:T(8,128)} %get-tuple-element.147), channel_id=1, source_target_pairs={{1,0},{2,1},{3,2},{5,4},{6,5},{7,6},{9,8},{10,9},{11,10},{13,12},{... | collective-permute-start | bytes 120968 | tf_op jit(solution)/shard_map/ppermute | solution.py:27
  137.5 1.5 collective-permute-start.10
  139.5 2.7 fusion.254
  144.6 5.4 %select_multiply_fusion = f32[4,8,16,257]{3,1,2,0:T(8,128)S(1)} fusion(f32[4,8,16,257]{3,2,1,0:T(8,128)} %get-tuple-element.88, f32[4,8,16,257]{3,2,1,0:T(8,128)S(1)} %get-tuple-element.84, f32[4,8,16,257]{3,2,1,0:T(8,128)} %get-tuple-element.85, f32[4,8,16,257]{3,2,1,0:T(8,128)} %get-tuple-element.86, f32[4,8,16,257]{3,2,1,0:T(8,128)} %get-tuple-element.87, ...), kind=kLoop, calls=%fused_computation.6 | loop fusion | flops 16579584 | bytes 3848832 | tf_op jit(solution)/shard_map/mul | solution.py:82
  154.4 1.6 fusion.255
  158.0 1.8 fusion.50
  159.8 3.7 %select_multiply_fusion.1 = f32[4,8,17,256]{3,1,2,0:T(8,128)S(1)} fusion(f32[4,8,17,256]{3,1,0,2:T(8,128)} %get-tuple-element.94, f32[4,8,17,256]{3,1,0,2:T(8,128)S(1)} %get-tuple-element.90, f32[4,8,17,256]{3,1,0,2:T(8,128)} %get-tuple-element.91, f32[4,8,17,256]{3,1,0,2:T(8,128)} %get-tuple-element.92, f32[4,8,17,256]{3,1,0,2:T(8,128)} %get-tuple-element.93, ...), kind=kLoop, calls=%fused_computation.40 | loop fusion | flops 17547264 | bytes 4073472 | tf_op jit(solution)/shard_map/mul | solution.py:82
  164.5 3.4 %collective-permute-start.5 = (f32[3,16,12]{2,1,0:T(8,128)S(1)}, f32[3,16,12]{2,1,0:T(8,128)S(1)}, u32[]{:S(2)}, u32[]{:S(2)}) collective-permute-start(f32[3,16,12]{2,1,0:T(8,128)S(1)} %get-tuple-element.155), channel_id=1, source_target_pairs={{4,0},{8,4},{12,8},{16,12},{20,16},{24,20},{28,24},{0,28},{5,1},{9... | collective-permute-start | bytes 6920 | tf_op jit(solution)/shard_map/ppermute | solution.py:27
  167.9 24.6 %all_gather.13 = f32[3,12,2048]{2,1,0:T(8,128)S(1)} all-gather(f32[3,12,256]{2,1,0:T(8,128)S(1)} %slice.1154), channel_id=1, replica_groups=mesh['lon'=8,'lat'=4] {'lon'}, dimensions={2}, use_global_device_ids=true | all-gather | bytes 331776 | tf_op jit(solution)/shard_map/all_gather | solution.py:110
  192.5 3.1 %copy.212 = f32[3,12,2048]{1,0,2:T(4,128)} copy(f32[3,12,2048]{2,1,0:T(8,128)S(1)} %all_gather.13) | data formatting | bytes 589824 | tf_op jit(solution)/shard_map/all_gather | solution.py:110
  195.7 12.0 %rev.24 = f32[3,12,2048]{1,0,2:T(4,128)} reverse(f32[3,12,2048]{1,0,2:T(4,128)} %copy.212), dimensions={1} | reverse | bytes 589824 | tf_op jit(solution)/shard_map/jit(_flip)/rev | solution.py:90
  207.7 3.3 %gather_fusion.1 = f32[280,3,12]{2,1,0:T(4,128)S(1)} fusion(f32[3,12,2048]{1,0,2:T(4,128)} %rev.24, s32[1024]{0:T(1024)S(1)} %copy-done.29), kind=kCustom, calls=%fused_computation.clone | custom fusion | bytes 81760 | tf_op jit(solution)/shard_map/jit(_take)/gather | solution.py:90
  214.5 9.8 %collective-permute-start.7 = (f32[3,12,280]{2,1,0:T(8,128)S(1)}, f32[3,12,280]{2,1,0:T(8,128)S(1)}, u32[]{:S(2)}, u32[]{:S(2)}) collective-permute-start(f32[3,12,280]{2,1,0:T(8,128)S(1)} %get-tuple-element.149), channel_id=1, source_target_pairs={{1,0},{2,1},{3,2},{5,4},{6,5},{7,6},{9,8},{10,9},{11,10},{13,12},{... | collective-permute-start | bytes 120968 | tf_op jit(solution)/shard_map/ppermute | solution.py:27
  224.3 1.5 collective-permute-start.6
  229.9 4.4 %collective-permute-start.13 = (f32[3,16,12]{2,1,0:T(8,128)S(1)}, f32[3,16,12]{2,1,0:T(8,128)S(1)}, u32[]{:S(2)}, u32[]{:S(2)}) collective-permute-start(f32[3,16,12]{2,1,0:T(8,128)S(1)} %get-tuple-element.151), channel_id=1, source_target_pairs={{4,0},{8,4},{12,8},{16,12},{20,16},{24,20},{28,24},{0,28},{5,1},{9... | collective-permute-start | bytes 6920 | tf_op jit(solution)/shard_map/ppermute | solution.py:27
  234.3 24.7 %all_gather.15 = f32[3,12,2048]{2,1,0:T(8,128)S(1)} all-gather(f32[3,12,256]{2,1,0:T(8,128)S(1)} %slice.1266), channel_id=1, replica_groups=mesh['lon'=8,'lat'=4] {'lon'}, dimensions={2}, use_global_device_ids=true | all-gather | bytes 331776 | tf_op jit(solution)/shard_map/all_gather | solution.py:110
  259.1 3.1 %copy.216 = f32[3,12,2048]{1,0,2:T(4,128)} copy(f32[3,12,2048]{2,1,0:T(8,128)S(1)} %all_gather.15) | data formatting | bytes 589824 | tf_op jit(solution)/shard_map/all_gather | solution.py:110
  262.2 12.0 %rev.26 = f32[3,12,2048]{1,0,2:T(4,128)} reverse(f32[3,12,2048]{1,0,2:T(4,128)} %copy.216), dimensions={1} | reverse | bytes 589824 | tf_op jit(solution)/shard_map/jit(_flip)/rev | solution.py:90
  274.2 3.2 %gather_fusion.3 = f32[280,3,12]{2,1,0:T(4,128)S(1)} fusion(f32[3,12,2048]{1,0,2:T(4,128)} %rev.26, s32[1024]{0:T(1024)S(1)} %copy-done.29), kind=kCustom, calls=%fused_computation.2.clone | custom fusion | bytes 81760 | tf_op jit(solution)/shard_map/jit(_take)/gather | solution.py:90
  277.5 10.9 %collective-permute-start.15 = (f32[3,12,280]{2,1,0:T(8,128)S(1)}, f32[3,12,280]{2,1,0:T(8,128)S(1)}, u32[]{:S(2)}, u32[]{:S(2)}) collective-permute-start(f32[3,12,280]{2,1,0:T(8,128)S(1)} %get-tuple-element.145), channel_id=1, source_target_pairs={{1,0},{2,1},{3,2},{5,4},{6,5},{7,6},{9,8},{10,9},{11,10},{13,12},{... | collective-permute-start | bytes 120968 | tf_op jit(solution)/shard_map/ppermute | solution.py:27
  288.5 1.3 collective-permute-start.14
  (237 shorter events, 43.9 us)
Async XLA Ops:
  0.6 54.2 %copy-start.4 = (f32[8,16,256]{2,1,0:T(8,128)S(1)}, f32[8,16,256]{2,1,0:T(8,128)}, u32[]{:S(2)}) copy-start(f32[8,16,256]{2,1,0:T(8,128)} %param.13) | copy-start | bytes 393220
  0.6 54.2 %copy-start.6 = (f32[8,16,256]{2,1,0:T(8,128)S(1)}, f32[8,16,256]{2,1,0:T(8,128)}, u32[]{:S(2)}) copy-start(f32[8,16,256]{2,1,0:T(8,128)} %param.14) | copy-start | bytes 393220
  0.7 54.2 %copy-start.8 = (f32[8,16,256]{2,1,0:T(8,128)S(1)}, f32[8,16,256]{2,1,0:T(8,128)}, u32[]{:S(2)}) copy-start(f32[8,16,256]{2,1,0:T(8,128)} %param.15) | copy-start | bytes 393220
  0.7 54.2 %copy-start.10 = (f32[8,16,256]{2,1,0:T(8,128)S(1)}, f32[8,16,256]{2,1,0:T(8,128)}, u32[]{:S(2)}) copy-start(f32[8,16,256]{2,1,0:T(8,128)} %param.16) | copy-start | bytes 393220
  0.7 48.4 %copy-start.22 = (s32[16,256]{1,0:T(8,128)S(1)}, s32[16,256]{1,0:T(8,128)}, u32[]{:S(2)}) copy-start(s32[16,256]{1,0:T(8,128)} %param.20) | copy-start | bytes 49156
  0.7 46.0 %copy-start.47 = (s32[256]{0:T(256)S(1)}, s32[256]{0:T(256)}, u32[]{:S(2)}) copy-start(s32[256]{0:T(256)} %param.21) | copy-start | bytes 3076
  6.2 143.8 %collective-permute-start.3 = (f32[33,3,256]{2,0,1:T(8,128)}, f32[33,3,256]{2,0,1:T(8,128)}, u32[]{:S(2)}, u32[]{:S(2)}) collective-permute-start(f32[33,3,256]{2,0,1:T(8,128)} %get-tuple-element.96), channel_id=1, source_target_pairs={{1,0},{2,1},{3,2},{5,4},{6,5},{7,6},{9,8},{10,9},{11,10},{13,12},{... | collective-permute-start | bytes 304136 | tf_op jit(solution)/shard_map/ppermute | solution.py:27
  9.5 141.6 %collective-permute-start.2 = (f32[33,3,256]{2,0,1:T(8,128)}, f32[33,3,256]{2,0,1:T(8,128)}, u32[]{:S(2)}, u32[]{:S(2)}) collective-permute-start(f32[33,3,256]{2,0,1:T(8,128)} %get-tuple-element.95), channel_id=1, source_target_pairs={{0,1},{1,2},{2,3},{4,5},{5,6},{6,7},{8,9},{9,10},{10,11},{12,13},{... | collective-permute-start | bytes 304136 | tf_op jit(solution)/shard_map/ppermute | solution.py:25
  10.9 126.7 %collective-permute-start.1 = (f32[33,16,3]{2,1,0:T(8,128)S(1)}, f32[33,16,3]{2,1,0:T(8,128)S(1)}, u32[]{:S(2)}, u32[]{:S(2)}) collective-permute-start(f32[33,16,3]{2,1,0:T(8,128)S(1)} %get-tuple-element.104), channel_id=1, source_target_pairs={{4,0},{8,4},{12,8},{16,12},{20,16},{24,20},{28,24},{0,28},{5,1},{9... | collective-permute-start | bytes 19016 | tf_op jit(solution)/shard_map/ppermute | solution.py:27
  16.7 103.8 %collective-permute-start.9 = (f32[3,16,12]{2,1,0:T(8,128)}, f32[3,16,12]{2,1,0:T(8,128)S(1)}, u32[]{:S(2)}, u32[]{:S(2)}) collective-permute-start(f32[3,16,12]{2,1,0:T(8,128)} %get-tuple-element.153), channel_id=1, source_target_pairs={{4,0},{8,4},{12,8},{16,12},{20,16},{24,20},{28,24},{0,28},{5,1},{9... | collective-permute-start | bytes 6920 | tf_op jit(solution)/shard_map/ppermute | solution.py:27
  16.9 103.6 %collective-permute-start.8 = (f32[3,16,12]{2,1,0:T(8,128)}, f32[3,16,12]{2,1,0:T(8,128)}, u32[]{:S(2)}, u32[]{:S(2)}) collective-permute-start(f32[3,16,12]{2,1,0:T(8,128)} %get-tuple-element.152), channel_id=1, source_target_pairs={{0,4},{4,8},{8,12},{12,16},{16,20},{20,24},{24,28},{28,0},{1,5},{5... | collective-permute-start | bytes 6920 | tf_op jit(solution)/shard_map/ppermute | solution.py:25
  81.9 34.5 %copy-start.28 = (s32[1024]{0:T(1024)}, s32[1024]{0:T(1024)S(1)}, u32[]{:S(2)}) copy-start(s32[1024]{0:T(1024)S(1)} %pad_clamp_fusion) | copy-start | bytes 12292
  120.5 19.0 %copy-start.26 = (f32[3,16,12]{2,1,0:T(8,128)}, f32[3,16,12]{2,1,0:T(8,128)S(1)}, u32[]{:S(2)}) copy-start(f32[3,16,12]{2,1,0:T(8,128)S(1)} %collective-permute-done.9) | copy-start | bytes 6916
  120.5 18.5 %collective-permute-start = (f32[33,16,3]{2,1,0:T(8,128)S(1)}, f32[33,16,3]{2,1,0:T(8,128)S(1)}, u32[]{:S(2)}, u32[]{:S(2)}) collective-permute-start(f32[33,16,3]{2,1,0:T(8,128)S(1)} %get-tuple-element.103), channel_id=1, source_target_pairs={{0,4},{4,8},{8,12},{12,16},{16,20},{20,24},{24,28},{28,0},{1,5},{5... | collective-permute-start | bytes 19016 | tf_op jit(solution)/shard_map/ppermute | solution.py:25
  122.0 90.3 %collective-permute-start.11 = (f32[3,12,280]{2,1,0:T(8,128)}, f32[3,12,280]{2,1,0:T(8,128)}, u32[]{:S(2)}, u32[]{:S(2)}) collective-permute-start(f32[3,12,280]{2,1,0:T(8,128)} %get-tuple-element.147), channel_id=1, source_target_pairs={{1,0},{2,1},{3,2},{5,4},{6,5},{7,6},{9,8},{10,9},{11,10},{13,12},{... | collective-permute-start | bytes 120968 | tf_op jit(solution)/shard_map/ppermute | solution.py:27
  137.5 75.8 %collective-permute-start.10 = (f32[3,12,280]{2,1,0:T(8,128)}, f32[3,12,280]{2,1,0:T(8,128)}, u32[]{:S(2)}, u32[]{:S(2)}) collective-permute-start(f32[3,12,280]{2,1,0:T(8,128)} %get-tuple-element.146), channel_id=1, source_target_pairs={{0,1},{1,2},{2,3},{4,5},{5,6},{6,7},{8,9},{9,10},{10,11},{12,13},{... | collective-permute-start | bytes 120968 | tf_op jit(solution)/shard_map/ppermute | solution.py:25
  164.5 49.9 %collective-permute-start.5 = (f32[3,16,12]{2,1,0:T(8,128)S(1)}, f32[3,16,12]{2,1,0:T(8,128)S(1)}, u32[]{:S(2)}, u32[]{:S(2)}) collective-permute-start(f32[3,16,12]{2,1,0:T(8,128)S(1)} %get-tuple-element.155), channel_id=1, source_target_pairs={{4,0},{8,4},{12,8},{16,12},{20,16},{24,20},{28,24},{0,28},{5,1},{9... | collective-permute-start | bytes 6920 | tf_op jit(solution)/shard_map/ppermute | solution.py:27
  167.9 46.5 %collective-permute-start.4 = (f32[3,16,12]{2,1,0:T(8,128)S(1)}, f32[3,16,12]{2,1,0:T(8,128)S(1)}, u32[]{:S(2)}, u32[]{:S(2)}) collective-permute-start(f32[3,16,12]{2,1,0:T(8,128)S(1)} %get-tuple-element.154), channel_id=1, source_target_pairs={{0,4},{4,8},{8,12},{12,16},{16,20},{20,24},{24,28},{28,0},{1,5},{5... | collective-permute-start | bytes 6920 | tf_op jit(solution)/shard_map/ppermute | solution.py:25
  195.6 17.7 %copy-start.15 = (f32[16,256]{1,0:T(8,128)S(1)}, f32[16,256]{1,0:T(8,128)}, u32[]{:S(2)}) copy-start(f32[16,256]{1,0:T(8,128)} %param.19) | copy-start | bytes 49156
  195.7 17.7 %copy-start.17 = (f32[16,256]{1,0:T(8,128)S(1)}, f32[16,256]{1,0:T(8,128)}, u32[]{:S(2)}) copy-start(f32[16,256]{1,0:T(8,128)} %param.18) | copy-start | bytes 49156
  195.7 17.7 %copy-start.25 = (f32[16,256]{1,0:T(8,128)S(1)}, f32[16,256]{1,0:T(8,128)}, u32[]{:S(2)}) copy-start(f32[16,256]{1,0:T(8,128)} %param.17) | copy-start | bytes 49156
  195.7 17.7 %copy-start.27 = (f32[3,16,12]{2,1,0:T(8,128)S(1)}, f32[3,16,12]{2,1,0:T(8,128)}, u32[]{:S(2)}) copy-start(f32[3,16,12]{2,1,0:T(8,128)} %copy-done.26) | copy-start | bytes 6916
  195.7 18.7 %copy-start.19 = (f32[1,16,256]{2,1,0:T(8,128)S(1)}, f32[1,16,256]{2,1,0:T(8,128)}, u32[]{:S(2)}) copy-start(f32[1,16,256]{2,1,0:T(8,128)} %get-tuple-element.160) | copy-start | bytes 49156
  207.7 20.1 %copy-start.42 = (f32[36]{0:T(128)S(1)}, f32[36]{0:T(128)}, u32[]{:S(2)}) copy-start(f32[36]{0:T(128)} %get-tuple-element.176) | copy-start | bytes 436
  207.7 20.1 %copy-start.43 = (f32[36]{0:T(128)S(1)}, f32[36]{0:T(128)}, u32[]{:S(2)}) copy-start(f32[36]{0:T(128)} %get-tuple-element.177) | copy-start | bytes 436
  211.0 17.3 %copy-start.40 = (f32[32]{0:T(128)S(1)}, f32[32]{0:T(128)}, u32[]{:S(2)}) copy-start(f32[32]{0:T(128)} %get-tuple-element.174) | copy-start | bytes 388
  214.5 13.0 %collective-permute-start.7 = (f32[3,12,280]{2,1,0:T(8,128)S(1)}, f32[3,12,280]{2,1,0:T(8,128)S(1)}, u32[]{:S(2)}, u32[]{:S(2)}) collective-permute-start(f32[3,12,280]{2,1,0:T(8,128)S(1)} %get-tuple-element.149), channel_id=1, source_target_pairs={{1,0},{2,1},{3,2},{5,4},{6,5},{7,6},{9,8},{10,9},{11,10},{13,12},{... | collective-permute-start | bytes 120968 | tf_op jit(solution)/shard_map/ppermute | solution.py:27
  224.3 3.2 %collective-permute-start.6 = (f32[3,12,280]{2,1,0:T(8,128)S(1)}, f32[3,12,280]{2,1,0:T(8,128)S(1)}, u32[]{:S(2)}, u32[]{:S(2)}) collective-permute-start(f32[3,12,280]{2,1,0:T(8,128)S(1)} %get-tuple-element.148), channel_id=1, source_target_pairs={{0,1},{1,2},{2,3},{4,5},{5,6},{6,7},{8,9},{9,10},{10,11},{12,13},{... | collective-permute-start | bytes 120968 | tf_op jit(solution)/shard_map/ppermute | solution.py:25
  229.9 47.5 %collective-permute-start.13 = (f32[3,16,12]{2,1,0:T(8,128)S(1)}, f32[3,16,12]{2,1,0:T(8,128)S(1)}, u32[]{:S(2)}, u32[]{:S(2)}) collective-permute-start(f32[3,16,12]{2,1,0:T(8,128)S(1)} %get-tuple-element.151), channel_id=1, source_target_pairs={{4,0},{8,4},{12,8},{16,12},{20,16},{24,20},{28,24},{0,28},{5,1},{9... | collective-permute-start | bytes 6920 | tf_op jit(solution)/shard_map/ppermute | solution.py:27
  234.3 43.1 %collective-permute-start.12 = (f32[3,16,12]{2,1,0:T(8,128)S(1)}, f32[3,16,12]{2,1,0:T(8,128)S(1)}, u32[]{:S(2)}, u32[]{:S(2)}) collective-permute-start(f32[3,16,12]{2,1,0:T(8,128)S(1)} %get-tuple-element.150), channel_id=1, source_target_pairs={{0,4},{4,8},{8,12},{12,16},{16,20},{20,24},{24,28},{28,0},{1,5},{5... | collective-permute-start | bytes 6920 | tf_op jit(solution)/shard_map/ppermute | solution.py:25
  277.5 13.5 %collective-permute-start.15 = (f32[3,12,280]{2,1,0:T(8,128)S(1)}, f32[3,12,280]{2,1,0:T(8,128)S(1)}, u32[]{:S(2)}, u32[]{:S(2)}) collective-permute-start(f32[3,12,280]{2,1,0:T(8,128)S(1)} %get-tuple-element.145), channel_id=1, source_target_pairs={{1,0},{2,1},{3,2},{5,4},{6,5},{7,6},{9,8},{10,9},{11,10},{13,12},{... | collective-permute-start | bytes 120968 | tf_op jit(solution)/shard_map/ppermute | solution.py:27
  288.5 3.2 %collective-permute-start.14 = (f32[3,12,280]{2,1,0:T(8,128)S(1)}, f32[3,12,280]{2,1,0:T(8,128)S(1)}, u32[]{:S(2)}, u32[]{:S(2)}) collective-permute-start(f32[3,12,280]{2,1,0:T(8,128)S(1)} %get-tuple-element.144), channel_id=1, source_target_pairs={{0,1},{1,2},{2,3},{4,5},{5,6},{6,7},{8,9},{9,10},{10,11},{12,13},{... | collective-permute-start | bytes 120968 | tf_op jit(solution)/shard_map/ppermute | solution.py:25
  (32 other events, 311.5 us)
where the time goes:
time: 301 us; the launch traced here: 296 us
  blocking collectives  103 us (34%)
  local copies, waits for them, and re-layouts  91.7 us (30%)
  starting transfers between devices  58.6 us (19%)
  other arithmetic  39.2 us (13%)
    all_gather x3, blocking collectives, extend_wave(): lax.all_gather(stacked_fields[:, tile_rows - margin:, :], 'lon', axis=2,...  74.7 us
    ppermute x8, starting transfers between devices, extended_2(): lax.ppermute(head, axis, [((i + 1) % count, i) for i in range(ends)])  51.8 us
    rev x4, local copies, waits for them, and re-layouts, partner_fold(): picked = jnp.take(jnp.flip(tops, axis=1), facing, axis=2)  47.5 us
    all_gather x1, blocking collectives, extend_deep(): lax.all_gather(stacked_fields[:, tile_rows - 3:, :], 'lon', axis=2, tiled...  28.6 us
    gather x5, local copies, waits for them, and re-layouts, partner_fold(): picked = jnp.take(jnp.flip(tops, axis=1), facing, axis=2)  14.6 us
    mul x4, other arithmetic, face_fluxes(): COURANT * face_speed * jnp.where(face_speed >= 0.0, upwind, downwind)  10.5 us
    all_gather x3, local copies, waits for them, and re-layouts, extend_wave(): lax.all_gather(stacked_fields[:, tile_rows - margin:, :], 'lon', axis=2,...  9.4 us
    unnamed x106, local copies, waits for them, and re-layouts  6.88 us
  transfers between devices with their start and end apart: 16, of which 1 were waited for; matrix products, arithmetic and copies ran while one was open for 40% of the time, Pallas kernels for 0%

commit v1 on v0

v1 whole, which is shorter than its diff:
```python
import functools

import jax
import jax.numpy as jnp
from jax import lax
from jax.experimental import pallas as pl
from jax.experimental.pallas import tpu as pltpu
from jax.sharding import PartitionSpec as P

SUBSTEPS = 12
COURANT = 0.15
PRESSURE_GAIN = 0.1
CORIOLIS = 0.3
WAVE_MASS = 1.2
WAVE_MOMENTUM = 1.2
EPSILON = 1e-06

LANES = 128
SUB = 8
SLOT = 32
DEEP = 3
FIELDS = 4
MARGIN = 2 * SUBSTEPS


def lane_of(shape):
    return lax.broadcasted_iota(jnp.int32, shape, len(shape) - 1)


def wide_roll(values, offset):
    width = values.shape[-1]
    return pltpu.roll(values, (-offset) % width, values.ndim - 1)


def four_slots(parts, source_lane, lane):
    packed = None
    for k, part in enumerate(parts):
        moved = pltpu.roll(part, (SLOT * k - source_lane) % LANES, part.ndim - 1)
        packed = moved if packed is None else jnp.where(lane >= SLOT * k, moved, packed)
    return packed


def pack_kernel(u, v, t, s, sea, zonal, merid, tally, east, west):
    levels, rows, cols = u.shape
    lane = lane_of((SUB, LANES))
    lo, hi = slice(0, LANES), slice(cols - LANES, cols)
    for g in range(rows // SUB):
        row = slice(SUB * g, SUB * (g + 1))
        for out, where, first in ((east, hi, LANES - SLOT), (west, lo, 0)):
            for k in range(levels):
                parts = [q[k, row, where] for q in (u, v, t, s)]
                out[k, row, :] = four_slots(parts, first, lane)
            parts = [q[row, where] for q in (sea, zonal, merid)]
            parts.append(tally[row, where].astype(jnp.float32))
            out[levels, row, :] = four_slots(parts, first, lane)


def halo_tile(from_east, from_west, k, lane):
    east = pltpu.roll(from_east, (-SLOT * k) % LANES, 1)
    west = pltpu.roll(from_west, (LANES - SLOT - SLOT * k) % LANES, 1)
    return jnp.where(lane < SLOT, east, jnp.where(lane >= LANES - SLOT, west, 0.0))


def widen_kernel(
    u, v, t, s, sea, zonal, merid, tally, from_west, from_east, fields, flat, msg_a, msg_b
):
    levels, rows, cols = u.shape
    lane = lane_of((SUB, LANES))
    own, halo = slice(0, cols), slice(cols, cols + LANES)
    for g in range(rows // SUB):
        row = slice(SUB * g, SUB * (g + 1))
        for k, q in enumerate((u, v, t, s)):
            fields[k, row, :, own] = jnp.swapaxes(q[:, row, :], 0, 1)
            tiles = [halo_tile(from_east[i, row, :], from_west[i, row, :], k, lane) for i in range(levels)]
            fields[k, row, :, halo] = jnp.swapaxes(jnp.stack(tiles), 0, 1)
        for k, q in enumerate((sea, zonal, merid, tally)):
            flat[k, row, own] = q[row, :].astype(jnp.float32)
            flat[k, row, halo] = halo_tile(from_east[levels, row, :], from_west[levels, row, :], k, lane)
    even = lax.rem(lax.axis_index("lat"), 2) == 0

    def fill(msg, first):
        for k in range(FIELDS):
            for q in range(DEEP):
                msg[k * DEEP + q] = fields[k, first + q]
        msg[FIELDS * DEEP, 0:DEEP, :] = flat[3, first : first + DEEP, :]
        msg[FIELDS * DEEP, DEEP:SUB, :] = jnp.zeros((SUB - DEEP, flat.shape[2]), jnp.float32)

    @pl.when(even)
    def _():
        fill(msg_a, rows - DEEP)
        fill(msg_b, 0)

    @pl.when(jnp.logical_not(even))
    def _():
        fill(msg_a, 0)
        fill(msg_b, rows - DEEP)


def across_fold(near, far, offset, lane):
    cols = near.shape[1] - LANES
    count = cols // LANES
    tiles = [far[:, cols:]] + [far[:, LANES * i : LANES * (i + 1)] for i in range(count)]
    tiles += [near[:, LANES * i : LANES * (i + 1)] for i in range(count)] + [near[:, cols:]]
    back = LANES - 1 - lane
    tiles = [jnp.take_along_axis(x, back, axis=1) for x in tiles[::-1]]
    amount = cols + LANES - 1 - offset
    tile, part = lax.div(amount, LANES), lax.rem(amount, LANES)
    moved = []
    for k in range(count + 3):
        value = tiles[k]
        for first in range(1, count):
            value = jnp.where(tile == first + 1, tiles[k + first], value)
        moved.append(pltpu.roll(value, LANES - part, 1))
    keep = lane < LANES - part
    out = [jnp.where(keep, moved[k], moved[k + 1]) for k in range(count + 2)]
    last = jnp.where(lane < SLOT, out[count + 1], jnp.where(lane >= LANES - SLOT, out[0], 0.0))
    return jnp.concatenate(out[1 : count + 1] + [last], axis=1)


def weno_flux(speed, low2, low1, here, up1, up2, up3):
    ahead = speed >= 0.0
    a = jnp.where(ahead, low2, up3)
    b = jnp.where(ahead, low1, up2)
    c = jnp.where(ahead, here, up1)
    d = jnp.where(ahead, up1, here)
    e = jnp.where(ahead, up2, low1)
    g0, g1, g2, g3 = b - a, c - b, d - c, e - d
    third = 13.0 / 3.0

    def smooth(curve, slope):
        total = (4.0 * EPSILON + slope * slope) + third * (curve * curve)
        return total * total

    q0 = smooth(g1 - g0, 3.0 * g1 - g0)
    q1 = smooth(g2 - g1, g1 + g2)
    q2 = smooth(g3 - g2, g3 - 3.0 * g2)
    w0 = q1 * q2
    w1 = 6.0 * (q0 * q2)
    w2 = 3.0 * (q0 * q1)
    top = w0 * (5.0 * g1 - 2.0 * g0) + w1 * (g1 + 2.0 * g2) + w2 * (4.0 * g2 - g3)
    face = c + top / (6.0 * (w0 + w1 + w2))
    return COURANT * speed * face


def level_sums(values, level, upwards):
    for step in (1, 2, 4):
        moved = pltpu.roll(values, SUB - step if upwards else step, 0)
        inside = level < SUB - step if upwards else level >= step
        values = values + jnp.where(inside, moved, 0.0)
    return values


def flux_kernel(
    sizes,
    seam,
    fields,
    flat,
    got_a,
    got_b,
    got_c,
    tracer_t,
    tracer_s,
    base_u,
    base_v,
    six,
    south,
    north,
    wet,
    speed_n,
    speed_e,
    flux_n,
    press,
    final,
):
    rows, lat_size = sizes
    cols = tracer_t.shape[2]
    width = cols + LANES
    lat = lax.axis_index("lat")
    even = lax.rem(lat, 2) == 0
    top = lat == lat_size - 1
    lane = lane_of((SUB, LANES))
    planes = FIELDS * DEEP

    @pl.when(even)
    def _():
        south[...] = got_b[...]
        north[...] = got_a[...]

    @pl.when(jnp.logical_not(even))
    def _():
        south[...] = got_a[...]

    @pl.when(jnp.logical_not(even) & jnp.logical_not(top))
    def _():
        north[...] = got_b[...]

    @pl.when(top)
    def _():
        offset = lax.rem(seam[0], cols)
        for k in range(FIELDS):
            for q in range(DEEP):
                ghost = across_fold(got_b[k * DEEP + q], got_c[k * DEEP + q], offset, lane)
                north[k * DEEP + DEEP - 1 - q] = -ghost if k < 2 else ghost
        ghost = across_fold(got_b[planes], got_c[planes], offset, lane)
        north[planes, 0:1, :] = ghost[DEEP - 1 : DEEP, :]

    def row_of(k, j, at):
        if j < DEEP:
            return south[k * DEEP + j, :, at]
        if j < DEEP + rows:
            return fields[k, j - DEEP, :, at]
        return north[k * DEEP + j - DEEP - rows, :, at]

    level = lax.broadcasted_iota(jnp.int32, (SUB, width), 0)
    level_real = level.astype(jnp.float32)
    every = slice(None)

    def set_wet(index, tally_row):
        wet[index] = (level_real < jnp.broadcast_to(tally_row, (SUB, width))).astype(jnp.float32)

    set_wet(0, south[planes, DEEP - 1 : DEEP, :])
    for j in range(rows):
        set_wet(j + 1, flat[3, j : j + 1, :])
    set_wet(rows + 1, north[planes, 0:1, :])

    for j in range(rows + 1):
        speed = row_of(1, j + 2, every) + row_of(1, j + 3, every)
        speed_n[j] = 0.5 * speed * wet[j] * wet[j + 1]
    for j in range(rows + 2):
        density = 0.8 * row_of(3, j + 2, every) - 0.2 * row_of(2, j + 2, every)
        press[j] = level_sums(density, level, False) - 0.5 * density

    def north_fluxes(index, carry):
        k, tile = lax.div(index, width // LANES), lax.rem(index, width // LANES)
        at = pl.ds(pl.multiple_of(tile * LANES, LANES), LANES)
        window = [row_of(k, j, at) for j in range(5)]
        for j in range(rows + 1):
            window.append(row_of(k, j + 5, at))
            flux_n[k, j, :, at] = weno_flux(speed_n[j, :, at], *window)
            window.pop(0)
        return carry

    lax.fori_loop(0, FIELDS * (width // LANES), north_fluxes, 0)

    total_rows = rows * lat_size

    def one_row(j, carry):
        mask = wet[j + 1]
        u = fields[0, j]
        speed = 0.5 * (u + wide_roll(u, 1)) * mask * wide_roll(mask, 1)
        spread = speed - wide_roll(speed, -1) + (speed_n[j + 1] - speed_n[j])
        upward = -level_sums(spread, level, True)
        rise = jnp.where(level >= 1, (0.5 * COURANT) * upward, 0.0)
        rates = []
        for k in range(FIELDS):
            q = fields[k, j]
            flux = weno_flux(
                speed,
                wide_roll(q, -2),
                wide_roll(q, -1),
                q,
                wide_roll(q, 1),
                wide_roll(q, 2),
                wide_roll(q, 3),
            )
            vertical = rise * (q + pltpu.roll(q, 1, 0))
            below = pltpu.roll(vertical, SUB - 1, 0)
            rates.append(
                -(flux - wide_roll(flux, -1))
                - (flux_n[k, j + 1] - flux_n[k, j])
                - (vertical - below)
            )
        place = (lat * rows + j).astype(jnp.float32)
        coriolis = CORIOLIS * (2.0 * (place + 0.5) / total_rows - 1.0)
        v = fields[1, j]
        pressure = press[j + 1]
        grad_east = 0.5 * (wide_roll(pressure, 1) - wide_roll(pressure, -1))
        grad_north = 0.5 * (press[j + 2] - press[j])
        force_u = rates[0] + coriolis * v - PRESSURE_GAIN * grad_east
        force_v = rates[1] - coriolis * u - PRESSURE_GAIN * grad_north
        depth = jnp.maximum(flat[3, pl.ds(j, 1), :], 1.0)
        six[4, pl.ds(j, 1), :] = jnp.sum(mask * force_u, axis=0, keepdims=True) / depth
        six[5, pl.ds(j, 1), :] = jnp.sum(mask * force_v, axis=0, keepdims=True) / depth
        base_u[j] = (u + force_u)[:, :cols]
        base_v[j] = (v + force_v)[:, :cols]
        for k in (2, 3):
            final[k - 2, j] = (mask * (fields[k, j] + rates[k]))[:, :cols]
        return carry

    lax.fori_loop(0, rows, one_row, 0)
    for g in range(rows // SUB):
        row = slice(SUB * g, SUB * (g + 1))
        tracer_t[:, row, :] = jnp.swapaxes(final[0, row], 0, 1)
        tracer_s[:, row, :] = jnp.swapaxes(final[1, row], 0, 1)
    six[0:4] = flat[...]


def pair_kernel(sizes, six, got_a, msg_1, msg_2):
    rows, lat_size = sizes
    lat = lax.axis_index("lat")
    even = lax.rem(lat, 2) == 0
    pair_even = lax.rem(lax.div(lat, 2), 2) == 0
    rest = MARGIN - rows

    def last(msg, lower, upper):
        msg[:, 0:rest, :] = lower[:, rows - rest : rows, :]
        msg[:, rest:MARGIN, :] = upper[...]

    def first(msg, lower, upper):
        msg[:, 0:rows, :] = lower[...]
        msg[:, rows:MARGIN, :] = upper[:, 0:rest, :]

    for bottom, lower, upper in ((True, six, got_a), (False, got_a, six)):
        for which in (True, False):
            here = (even if bottom else jnp.logical_not(even)) & (
                pair_even if which else jnp.logical_not(pair_even)
            )

            @pl.when(here)
            def _(lower=lower, upper=upper, which=which):
                (last if which else first)(msg_1, lower, upper)
                (first if which else last)(msg_2, lower, upper)


def wave_kernel(
    sizes,
    seam,
    six,
    got_a,
    got_1,
    got_2,
    got_f,
    base_u,
    base_v,
    out_u,
    out_v,
    out_sea,
    out_zonal,
    out_merid,
    space,
):
    rows, levels, lat_size = sizes
    cols = out_sea.shape[1]
    width = cols + LANES
    lat = lax.axis_index("lat")
    even = lax.rem(lat, 2) == 0
    pair = lax.div(lat, 2)
    pair_even = lax.rem(pair, 2) == 0
    top = pair == lat_size // 2 - 1
    lane = lane_of((SUB, LANES))
    own_low = slice(MARGIN, MARGIN + rows)
    own_high = slice(MARGIN + rows, MARGIN + 2 * rows)
    below, above = slice(0, MARGIN), slice(MARGIN + 2 * rows, 2 * MARGIN + 2 * rows)

    @pl.when(even)
    def _():
        space[:, own_low, :] = six[...]
        space[:, own_high, :] = got_a[...]

    @pl.when(jnp.logical_not(even))
    def _():
        space[:, own_low, :] = got_a[...]
        space[:, own_high, :] = six[...]

    @pl.when(pair_even)
    def _():
        space[:, below, :] = got_2[...]
        space[:, above, :] = got_1[...]

    @pl.when(jnp.logical_not(pair_even))
    def _():
        space[:, below, :] = got_1[...]

    @pl.when(jnp.logical_not(pair_even) & jnp.logical_not(top))
    def _():
        space[:, above, :] = got_2[...]

    @pl.when(top)
    def _():
        offset = lax.rem(seam[0], cols)
        turn = SUB - 1 - lax.broadcasted_iota(jnp.int32, (SUB, LANES), 0)
        for k, parity in enumerate((1.0, -1.0, -1.0, 1.0, -1.0, -1.0)):
            for g in range(MARGIN // SUB):
                row = slice(SUB * g, SUB * (g + 1))
                ghost = across_fold(got_2[k, row, :], got_f[k, row, :], offset, lane)
                place = above.start + MARGIN - SUB * (g + 1)
                for i in range(width // LANES):
                    part = jnp.take_along_axis(ghost[:, LANES * i : LANES * (i + 1)], turn, axis=0)
                    space[k, place : place + SUB, LANES * i : LANES * (i + 1)] = parity * part

    height = rows + 2 * MARGIN
    window = pl.ds(pl.multiple_of(jnp.where(even, 0, rows), SUB), height)
    tally = space[3, window, :]
    wet = (tally > 0.0).astype(jnp.float32)
    thick = (0.5 * WAVE_MASS / levels) * tally
    total_rows = rows * lat_size
    place = lax.broadcasted_iota(jnp.int32, (height, width), 0) + (lat * rows - MARGIN)
    place = jnp.minimum(place, 2 * total_rows - 1 - place).astype(jnp.float32)
    turning = (CORIOLIS / SUBSTEPS) * (2.0 * (place + 0.5) / total_rows - 1.0)
    push_u = space[4, window, :] * (1.0 / SUBSTEPS)
    push_v = space[5, window, :] * (1.0 / SUBSTEPS)

    def step(index, state):
        sea, zonal, merid = state
        mass_e, mass_n = thick * zonal, thick * merid
        spread = (wide_roll(mass_e, 1) - wide_roll(mass_e, -1)) + (
            pltpu.roll(mass_n, height - 1, 0) - pltpu.roll(mass_n, 1, 0)
        )
        sea = wet * (sea - spread)
        slope_e = wide_roll(sea, 1) - wide_roll(sea, -1)
        slope_n = pltpu.roll(sea, height - 1, 0) - pltpu.roll(sea, 1, 0)
        half = 0.5 * WAVE_MOMENTUM
        next_zonal = wet * (zonal - half * slope_e + (turning * merid + push_u))
        next_merid = wet * (merid - half * slope_n + (push_v - turning * zonal))
        return sea, next_zonal, next_merid

    start = (space[0, window, :], space[1, window, :], space[2, window, :])
    sea, zonal, merid = lax.fori_loop(0, SUBSTEPS, step, start)
    mine = slice(MARGIN, MARGIN + rows)
    out_sea[...] = sea[mine, :cols]
    out_zonal[...] = zonal[mine, :cols]
    out_merid[...] = merid[mine, :cols]
    level = lax.broadcasted_iota(jnp.int32, (SUB, cols), 0).astype(jnp.float32)
    for base, flow, final, start_of, mean in (
        (base_u, out_u, out_zonal, 1, 4),
        (base_v, out_v, out_merid, 2, 5),
    ):
        for g in range(rows // SUB):
            block = []
            for j in range(SUB * g, SUB * (g + 1)):
                row = slice(j, j + 1)
                mask = level < jnp.broadcast_to(six[3, row, :cols], (SUB, cols))
                change = final[row, :] - six[start_of, row, :cols] - six[mean, row, :cols]
                block.append(mask.astype(jnp.float32) * (base[j] + jnp.broadcast_to(change, (SUB, cols))))
            flow[:, SUB * g : SUB * (g + 1), :] = jnp.swapaxes(jnp.stack(block), 0, 1)


def real(*shape):
    return jax.ShapeDtypeStruct(shape, jnp.float32)


def call(kernel, outs, scratch=(), seam=False):
    vmem = pl.BlockSpec(memory_space=pltpu.VMEM)

    def run(*args):
        specs = [vmem] * len(args)
        if seam:
            specs[0] = pl.BlockSpec(memory_space=pltpu.SMEM)
        return pl.pallas_call(
            kernel,
            out_shape=outs,
            in_specs=specs,
            out_specs=jax.tree.map(lambda _: vmem, outs),
            scratch_shapes=[pltpu.VMEM(shape, jnp.float32) for shape in scratch],
        )(*args)

    return run


def on_device(lon_size, lat_size, *arguments):
    u, v, t, s, sea, zonal, merid, tally, seam = arguments
    levels, rows, cols = u.shape
    width = cols + LANES
    assert levels == SUB and rows % SUB == 0 and lat_size % 4 == 0
    tile = lax.rem(lax.div(seam[0], cols) + lax.axis_index("lon"), lon_size)

    def moves(lats, fold=(), turn=0):
        pairs = [(x * lat_size + a, x * lat_size + b) for a, b in lats for x in range(lon_size)]
        for a in fold:
            pairs += [(x * lat_size + a, (turn - x) % lon_size * lat_size + a) for x in range(lon_size)]
        return pairs

    def send(values, pairs):
        return lax.ppermute(values, ("lon", "lat"), pairs)

    def both(pairs):
        return [p for a, b in pairs for p in ((a, b), (b, a))]

    ring = [(i, (i + 1) % lon_size) for i in range(lon_size)]
    inside = both((a, a + 1) for a in range(0, lat_size, 2))
    between = both((a, a + 1) for a in range(1, lat_size - 1, 2))
    chips = lat_size // 2
    chips_1 = both((2 * c + b, 2 * c + 2 + b) for c in range(0, chips - 1, 2) for b in (0, 1))
    chips_2 = both((2 * c + b, 2 * c + 2 + b) for c in range(1, chips - 1, 2) for b in (0, 1))
    last, last_two = (lat_size - 1,), (lat_size - 2, lat_size - 1)

    message = real(levels + 1, rows, LANES)
    flat_args = (u, v, t, s, sea, zonal, merid, tally)
    east, west = call(pack_kernel, (message, message))(*flat_args)
    from_west = lax.ppermute(east, "lon", ring)
    from_east = lax.ppermute(west, "lon", [(b, a) for a, b in ring])

    deep = real(FIELDS * DEEP + 1, SUB, width)
    fields, flat, msg_a, msg_b = call(
        widen_kernel,
        (real(FIELDS, rows, SUB, width), real(FIELDS, rows, width), deep, deep),
    )(*flat_args, from_west, from_east)

    def deep_exchange(turn):
        def run(a, b):
            return (
                send(a, moves(inside)),
                send(b, moves(between, last, turn)),
                send(b, moves((), last, turn - 1)),
            )

        return run

    got_a, got_b, got_c = lax.switch(tile, [deep_exchange(i) for i in range(lon_size)], msg_a, msg_b)

    base = real(rows, SUB, cols)
    tracer = real(levels, rows, cols)
    tracer_t, tracer_s, base_u, base_v, six = call(
        functools.partial(flux_kernel, (rows, lat_size)),
        (tracer, tracer, base, base, real(6, rows, width)),
        scratch=(
            deep.shape,
            deep.shape,
            (rows + 2, SUB, width),
            (rows + 1, SUB, width),
            (rows, SUB, width),
            (FIELDS, rows + 1, SUB, width),
            (rows + 2, SUB, width),
            (2, rows, SUB, cols),
        ),
        seam=True,
    )(seam, fields, flat, got_a, got_b, got_c)

    got_pair = send(six, moves(inside))
    strip = real(6, MARGIN, width)
    msg_1, msg_2 = call(functools.partial(pair_kernel, (rows, lat_size)), (strip, strip))(six, got_pair)

    def strip_exchange(turn):
        def run(a, b):
            return (
                send(a, moves(chips_1)),
                send(b, moves(chips_2, last_two, turn)),
                send(b, moves((), last_two, turn - 1)),
            )

        return run

    got_1, got_2, got_f = lax.switch(tile, [strip_exchange(i) for i in range(lon_size)], msg_1, msg_2)
    plane = real(rows, cols)
    out_u, out_v, out_sea, out_zonal, out_merid = call(
        functools.partial(wave_kernel, (rows, levels, lat_size)),
        (tracer, tracer, plane, plane, plane),
        scratch=((6, 2 * rows + 2 * MARGIN, width),),
        seam=True,
    )(seam, six, got_pair, got_1, got_2, got_f, base_u, base_v)
    return out_u, out_v, tracer_t, tracer_s, out_sea, out_zonal, out_merid


def solution(mesh):
    deep, plane = P(None, "lat", "lon"), P("lat", "lon")
    return jax.shard_map(
        functools.partial(on_device, mesh.shape["lon"], mesh.shape["lat"]),
        mesh=mesh,
        in_specs=(deep,) * 4 + (plane,) * 4 + (P("lon"),),
        out_specs=(deep,) * 4 + (plane,) * 3,
        check_vma=False,
    )
```

time: 301 us -> 60.6 us (0.20)
  the two profiles are of different devices: /device:TPU:3 before, /device:TPU:27 now
where the time goes in v1:
time: 60.6 us; the launch traced here: 61.5 us
  Pallas kernels  20.9 us (34%)
  waiting for transfers between devices  20.8 us (34%)
  starting transfers between devices  14.5 us (24%)
  between operations  2.62 us (4%)
  local copies, waits for them, and re-layouts  2.5 us (4%)
    pallas_call x5, Pallas kernels, run(): pl.pallas_call(kernel, out_shape=outs, in_specs=specs, out_specs=jax.tree...  20.9 us
    ppermute x7, waiting for transfers between devices, send(): return lax.ppermute(values, ('lon', 'lat'), pairs)  19.7 us
    ppermute x7, starting transfers between devices, send(): return lax.ppermute(values, ('lon', 'lat'), pairs)  12.2 us
    unnamed x8, local copies, waits for them, and re-layouts  1.98 us
    ppermute x1, starting transfers between devices, on_device(): from_west = lax.ppermute(east, 'lon', ring)  1.24 us
  transfers between devices with their start and end apart: 9, of which 7 were waited for; matrix products, arithmetic and copies ran while one was open for 1% of the time, Pallas kernels for 0%

profile of v1, /device:TPU:27, one launch (start us, length us, event | category | flops | bytes accessed | tf_op | source)
XLA Modules:
  0.0 61.5 jit_solution(18259295412721651591)
XLA Ops:
  0.6 1.9 %shard_map.144 = (f32[9,16,128]{2,1,0:T(8,128)}, f32[9,16,128]{2,1,0:T(8,128)}) custom-call(f32[8,16,256]{2,1,0:T(8,128)} %u.3, f32[8,16,256]{2,1,0:T(8,128)} %v.3, f32[8,16,256]{2,1,0:T(8,128)} %t.3, f32[8,16,256]{2,1,0:T(8,128)} %s.3, f32[16,256]{1,0:T(8,128)} %sea.3, f32[16,256]{1,0:T(8,128)} %zonal.3, f32[16,256]{1,0:T(8,128)} %merid.3, s32[16,256]{1,0:T(8,128)} %tally.3), custom_call_target="tpu_custom_call" | custom-call | tf_op jit(solution)/shard_map/pallas_call | solution.py:449
  2.6 1.2 %collective-permute-start.48 = (f32[9,16,128]{2,1,0:T(8,128)}, f32[9,16,128]{2,1,0:T(8,128)S(1)}, u32[]{:S(2)}, u32[]{:S(2)}) collective-permute-start(f32[9,16,128]{2,1,0:T(8,128)} %get-tuple-element.125), channel_id=1, source_target_pairs={{0,4},{4,8},{8,12},{12,16},{16,20},{20,24},{24,28},{28,0},{1,5},{5... | collective-permute-start | bytes 221192 | tf_op jit(solution)/shard_map/ppermute | solution.py:490
  3.8 1.1 %collective-permute-start.49 = (f32[9,16,128]{2,1,0:T(8,128)}, f32[9,16,128]{2,1,0:T(8,128)S(1)}, u32[]{:S(2)}, u32[]{:S(2)}) collective-permute-start(f32[9,16,128]{2,1,0:T(8,128)} %get-tuple-element.126), channel_id=1, source_target_pairs={{4,0},{8,4},{12,8},{16,12},{20,16},{24,20},{28,24},{0,28},{5,1},{9... | collective-permute-start | bytes 221192 | tf_op jit(solution)/shard_map/ppermute | solution.py:491
  4.9 0.0 copy-start.3
  4.9 0.7 %copy-done.3 = s32[256]{0:T(256)S(1)} copy-done((s32[256]{0:T(256)S(1)}, s32[256]{0:T(256)}, u32[]{:S(2)}) %copy-start.3) | copy-done | bytes 1048
  5.6 0.5 slice.3
  8.1 0.0 collective-permute-done.48.from_west
  8.1 0.0 copy-start.1
  8.1 1.1 %collective-permute-done.49.from_east = f32[9,16,128]{2,1,0:T(8,128)S(1)} collective-permute-done((f32[9,16,128]{2,1,0:T(8,128)}, f32[9,16,128]{2,1,0:T(8,128)S(1)}, u32[]{:S(2)}, u32[]{:S(2)}) %collective-permute-start.49) | collective-permute-done | bytes 73760 | tf_op jit(solution)/shard_map/ppermute | solution.py:491
  9.2 0.0 copy-done.1
  9.2 0.6 %copy-done.2 = f32[9,16,128]{2,1,0:T(8,128)} copy-done((f32[9,16,128]{2,1,0:T(8,128)}, f32[9,16,128]{2,1,0:T(8,128)S(1)}, u32[]{:S(2)}) %copy-start.2) | copy-done | bytes 73752
  9.8 2.4 %shard_map.145 = (f32[4,16,8,384]{3,2,1,0:T(8,128)}, f32[4,16,384]{2,1,0:T(8,128)}, f32[13,8,384]{2,1,0:T(8,128)S(1)}, f32[13,8,384]{2,1,0:T(8,128)S(1)}) custom-call(f32[8,16,256]{2,1,0:T(8,128)} %u.3, f32[8,16,256]{2,1,0:T(8,128)} %v.3, f32[8,16,256]{2,1,0:T(8,128)} %t.3, f32[8,16,256]{2,1,0:T(8,128)} %s.3, f32[16,256]{1,0:T(8,128)} %sea.3, ...), custom_call_target="tpu_custom_call" | custom-call | tf_op jit(solution)/shard_map/pallas_call | solution.py:449
  12.2 12.0 %conditional.2 = (f32[13,8,384]{2,1,0:T(8,128)}, f32[13,8,384]{2,1,0:T(8,128)}, f32[13,8,384]{2,1,0:T(8,128)}) conditional(s32[]{:T(128)} %clamp.4, (f32[13,8,384]{2,1,0:T(8,128)S(1)}, f32[13,8,384]{2,1,0:T(8,128)S(1)}) %tuple.64, (f32[13,8,384]{2,1,0:T(8,128)S(1)}, f32[13,8,384]{2,1,0:T(8,128)S(1)}) %tuple.64, ...), branch_computations={%region_0.0_spmd, %region_1.0_spmd, %region_2.0_spmd, %region_3.0_... | conditional | bytes 1917072 | solution.py:509
  12.2 0.8 %collective-permute-start.3 = (f32[13,8,384]{2,1,0:T(8,128)S(1)}, f32[13,8,384]{2,1,0:T(8,128)}, u32[]{:S(2)}, u32[]{:S(2)}) collective-permute-start(f32[13,8,384]{2,1,0:T(8,128)S(1)} %get-tuple-element.66), channel_id=1, source_target_pairs={{0,1},{4,5},{8,9},{12,13},{16,17},{20,21},{24,25},{28,29},{1,0},{5... | collective-permute-start | bytes 479240 | tf_op jit(solution)/shard_map/cond/branch_1_fun/ppermute | solution.py:474
  13.0 2.0 %collective-permute-start.5 = (f32[13,8,384]{2,1,0:T(8,128)S(1)}, f32[13,8,384]{2,1,0:T(8,128)}, u32[]{:S(2)}, u32[]{:S(2)}) collective-permute-start(f32[13,8,384]{2,1,0:T(8,128)S(1)} %get-tuple-element.67), channel_id=1, source_target_pairs={{3,3},{7,31},{11,27},{15,23},{19,19},{23,15},{27,11},{31,7}} | collective-permute-start | bytes 479240 | tf_op jit(solution)/shard_map/cond/branch_1_fun/ppermute | solution.py:474
  14.9 4.4 %collective-permute-start.4 = (f32[13,8,384]{2,1,0:T(8,128)S(1)}, f32[13,8,384]{2,1,0:T(8,128)}, u32[]{:S(2)}, u32[]{:S(2)}) collective-permute-start(f32[13,8,384]{2,1,0:T(8,128)S(1)} %get-tuple-element.67), channel_id=1, source_target_pairs={{1,2},{5,6},{9,10},{13,14},{17,18},{21,22},{25,26},{29,30},{2,1},{... | collective-permute-start | bytes 479240 | tf_op jit(solution)/shard_map/cond/branch_1_fun/ppermute | solution.py:474
  19.4 0.0 collective-permute-done.3
  19.4 0.6 collective-permute-done.5
  20.0 4.3 %collective-permute-done.4 = f32[13,8,384]{2,1,0:T(8,128)} collective-permute-done((f32[13,8,384]{2,1,0:T(8,128)S(1)}, f32[13,8,384]{2,1,0:T(8,128)}, u32[]{:S(2)}, u32[]{:S(2)}) %collective-permute-start.4) | collective-permute-done | bytes 159776 | tf_op jit(solution)/shard_map/cond/branch_1_fun/ppermute | solution.py:474
  24.3 8.9 %shard_map.146 = (f32[8,16,256]{2,1,0:T(8,128)}, f32[8,16,256]{2,1,0:T(8,128)}, f32[16,8,256]{2,1,0:T(8,128)}, f32[16,8,256]{2,1,0:T(8,128)}, f32[6,16,384]{2,1,0:T(8,128)}) custom-call(s32[256]{0:T(256)} %seam.3, f32[4,16,8,384]{3,2,1,0:T(8,128)} %get-tuple-element.127.fields, f32[4,16,384]{2,1,0:T(8,128)} %get-tuple-element.128.flat, ...), custom_call_target="tpu_custom_call" | custom-call | tf_op jit(solution)/shard_map/pallas_call | solution.py:449
  33.2 0.0 collective-permute-start.50
  33.2 1.6 %collective-permute-done.50.got_a = f32[6,16,384]{2,1,0:T(8,128)S(1)} collective-permute-done((f32[6,16,384]{2,1,0:T(8,128)}, f32[6,16,384]{2,1,0:T(8,128)S(1)}, u32[]{:S(2)}, u32[]{:S(2)}) %collective-permute-start.50) | collective-permute-done | bytes 147488 | tf_op jit(solution)/shard_map/ppermute | solution.py:474
  34.8 0.7 %copy-done = f32[6,16,384]{2,1,0:T(8,128)} copy-done((f32[6,16,384]{2,1,0:T(8,128)}, f32[6,16,384]{2,1,0:T(8,128)S(1)}, u32[]{:S(2)}) %copy-start) | copy-done | bytes 147480
  35.4 1.0 %shard_map.147 = (f32[6,24,384]{2,1,0:T(8,128)S(1)}, f32[6,24,384]{2,1,0:T(8,128)S(1)}) custom-call(f32[6,16,384]{2,1,0:T(8,128)} %get-tuple-element.134.six, f32[6,16,384]{2,1,0:T(8,128)} %copy-done), custom_call_target="tpu_custom_call" | custom-call | tf_op jit(solution)/shard_map/pallas_call | solution.py:449
  36.4 18.4 %conditional.3 = (f32[6,24,384]{2,1,0:T(8,128)}, f32[6,24,384]{2,1,0:T(8,128)}, f32[6,24,384]{2,1,0:T(8,128)}) conditional(s32[]{:T(128)} %clamp.4, (f32[6,24,384]{2,1,0:T(8,128)S(1)}, f32[6,24,384]{2,1,0:T(8,128)S(1)}) %shard_map.147, (f32[6,24,384]{2,1,0:T(8,128)S(1)}, f32[6,24,384]{2,1,0:T(8,128)S(1)}) %shard_map.147, ...), branch_computations={%region_8.0_spmd, %region_9.0_spmd, %region_10.0_spmd, %region_11.... | conditional | bytes 2654352 | solution.py:543
  36.5 0.1 collective-permute-start.27
  36.5 2.8 %collective-permute-start.29 = (f32[6,24,384]{2,1,0:T(8,128)S(1)}, f32[6,24,384]{2,1,0:T(8,128)}, u32[]{:S(2)}, u32[]{:S(2)}) collective-permute-start(f32[6,24,384]{2,1,0:T(8,128)S(1)} %get-tuple-element.83), channel_id=1, source_target_pairs={{2,2},{6,30},{10,26},{14,22},{18,18},{22,14},{26,10},{30,6},{3,3},... | collective-permute-start | bytes 663560 | tf_op jit(solution)/shard_map/cond/branch_1_fun/ppermute | solution.py:474
  39.4 2.1 %collective-permute-start.28 = (f32[6,24,384]{2,1,0:T(8,128)S(1)}, f32[6,24,384]{2,1,0:T(8,128)}, u32[]{:S(2)}, u32[]{:S(2)}) collective-permute-start(f32[6,24,384]{2,1,0:T(8,128)S(1)} %get-tuple-element.83), channel_id=1, source_target_pairs={{2,6},{6,2},{10,30},{14,26},{18,22},{22,18},{26,14},{30,10},{3,7},... | collective-permute-start | bytes 663560 | tf_op jit(solution)/shard_map/cond/branch_1_fun/ppermute | solution.py:474
  41.5 2.0 %collective-permute-done.27 = f32[6,24,384]{2,1,0:T(8,128)} collective-permute-done((f32[6,24,384]{2,1,0:T(8,128)S(1)}, f32[6,24,384]{2,1,0:T(8,128)}, u32[]{:S(2)}, u32[]{:S(2)}) %collective-permute-start.27) | collective-permute-done | bytes 221216 | tf_op jit(solution)/shard_map/cond/branch_1_fun/ppermute | solution.py:474
  43.5 2.8 %collective-permute-done.29 = f32[6,24,384]{2,1,0:T(8,128)} collective-permute-done((f32[6,24,384]{2,1,0:T(8,128)S(1)}, f32[6,24,384]{2,1,0:T(8,128)}, u32[]{:S(2)}, u32[]{:S(2)}) %collective-permute-start.29) | collective-permute-done | bytes 221216 | tf_op jit(solution)/shard_map/cond/branch_1_fun/ppermute | solution.py:474
  46.3 8.5 %collective-permute-done.28 = f32[6,24,384]{2,1,0:T(8,128)} collective-permute-done((f32[6,24,384]{2,1,0:T(8,128)S(1)}, f32[6,24,384]{2,1,0:T(8,128)}, u32[]{:S(2)}, u32[]{:S(2)}) %collective-permute-start.28) | collective-permute-done | bytes 221216 | tf_op jit(solution)/shard_map/cond/branch_1_fun/ppermute | solution.py:474
  54.8 6.7 %shard_map.148 = (f32[8,16,256]{2,1,0:T(8,128)}, f32[8,16,256]{2,1,0:T(8,128)}, f32[16,256]{1,0:T(8,128)}, f32[16,256]{1,0:T(8,128)}, f32[16,256]{1,0:T(8,128)}) custom-call(s32[256]{0:T(256)} %seam.3, f32[6,16,384]{2,1,0:T(8,128)} %get-tuple-element.134.six, f32[6,16,384]{2,1,0:T(8,128)} %copy-done, f32[6,24,384]{2,1,0:T(8,128)} %get-tuple-element.135.got_1, ...), custom_call_target="tpu_custom_call" | custom-call | tf_op jit(solution)/shard_map/pallas_call | solution.py:449
  (2 shorter events, 0.0 us)
Async XLA Ops:
  2.6 5.5 %collective-permute-start.48 = (f32[9,16,128]{2,1,0:T(8,128)}, f32[9,16,128]{2,1,0:T(8,128)S(1)}, u32[]{:S(2)}, u32[]{:S(2)}) collective-permute-start(f32[9,16,128]{2,1,0:T(8,128)} %get-tuple-element.125), channel_id=1, source_target_pairs={{0,4},{4,8},{8,12},{12,16},{16,20},{20,24},{24,28},{28,0},{1,5},{5... | collective-permute-start | bytes 221192 | tf_op jit(solution)/shard_map/ppermute | solution.py:490
  3.8 5.4 %collective-permute-start.49 = (f32[9,16,128]{2,1,0:T(8,128)}, f32[9,16,128]{2,1,0:T(8,128)S(1)}, u32[]{:S(2)}, u32[]{:S(2)}) collective-permute-start(f32[9,16,128]{2,1,0:T(8,128)} %get-tuple-element.126), channel_id=1, source_target_pairs={{4,0},{8,4},{12,8},{16,12},{20,16},{24,20},{28,24},{0,28},{5,1},{9... | collective-permute-start | bytes 221192 | tf_op jit(solution)/shard_map/ppermute | solution.py:491
  4.9 0.7 %copy-start.3 = (s32[256]{0:T(256)S(1)}, s32[256]{0:T(256)}, u32[]{:S(2)}) copy-start(s32[256]{0:T(256)} %seam.3) | copy-start | bytes 3076
  8.1 1.1 %copy-start.1 = (f32[9,16,128]{2,1,0:T(8,128)}, f32[9,16,128]{2,1,0:T(8,128)S(1)}, u32[]{:S(2)}) copy-start(f32[9,16,128]{2,1,0:T(8,128)S(1)} %collective-permute-done.48.from_west) | copy-start | bytes 221188
  9.2 0.6 %copy-start.2 = (f32[9,16,128]{2,1,0:T(8,128)}, f32[9,16,128]{2,1,0:T(8,128)S(1)}, u32[]{:S(2)}) copy-start(f32[9,16,128]{2,1,0:T(8,128)S(1)} %collective-permute-done.49.from_east) | copy-start | bytes 221188
  12.2 7.2 %collective-permute-start.3 = (f32[13,8,384]{2,1,0:T(8,128)S(1)}, f32[13,8,384]{2,1,0:T(8,128)}, u32[]{:S(2)}, u32[]{:S(2)}) collective-permute-start(f32[13,8,384]{2,1,0:T(8,128)S(1)} %get-tuple-element.66), channel_id=1, source_target_pairs={{0,1},{4,5},{8,9},{12,13},{16,17},{20,21},{24,25},{28,29},{1,0},{5... | collective-permute-start | bytes 479240 | tf_op jit(solution)/shard_map/cond/branch_1_fun/ppermute | solution.py:474
  13.0 7.0 %collective-permute-start.5 = (f32[13,8,384]{2,1,0:T(8,128)S(1)}, f32[13,8,384]{2,1,0:T(8,128)}, u32[]{:S(2)}, u32[]{:S(2)}) collective-permute-start(f32[13,8,384]{2,1,0:T(8,128)S(1)} %get-tuple-element.67), channel_id=1, source_target_pairs={{3,3},{7,31},{11,27},{15,23},{19,19},{23,15},{27,11},{31,7}} | collective-permute-start | bytes 479240 | tf_op jit(solution)/shard_map/cond/branch_1_fun/ppermute | solution.py:474
  14.9 9.3 %collective-permute-start.4 = (f32[13,8,384]{2,1,0:T(8,128)S(1)}, f32[13,8,384]{2,1,0:T(8,128)}, u32[]{:S(2)}, u32[]{:S(2)}) collective-permute-start(f32[13,8,384]{2,1,0:T(8,128)S(1)} %get-tuple-element.67), channel_id=1, source_target_pairs={{1,2},{5,6},{9,10},{13,14},{17,18},{21,22},{25,26},{29,30},{2,1},{... | collective-permute-start | bytes 479240 | tf_op jit(solution)/shard_map/cond/branch_1_fun/ppermute | solution.py:474
  33.2 1.6 %collective-permute-start.50 = (f32[6,16,384]{2,1,0:T(8,128)}, f32[6,16,384]{2,1,0:T(8,128)S(1)}, u32[]{:S(2)}, u32[]{:S(2)}) collective-permute-start(f32[6,16,384]{2,1,0:T(8,128)} %get-tuple-element.134.six), channel_id=1, source_target_pairs={{0,1},{4,5},{8,9},{12,13},{16,17},{20,21},{24,25},{28,29},{1,0},{5... | collective-permute-start | bytes 442376 | tf_op jit(solution)/shard_map/ppermute | solution.py:474
  34.8 0.7 %copy-start = (f32[6,16,384]{2,1,0:T(8,128)}, f32[6,16,384]{2,1,0:T(8,128)S(1)}, u32[]{:S(2)}) copy-start(f32[6,16,384]{2,1,0:T(8,128)S(1)} %collective-permute-done.50.got_a) | copy-start | bytes 442372
  36.5 7.0 %collective-permute-start.27 = (f32[6,24,384]{2,1,0:T(8,128)S(1)}, f32[6,24,384]{2,1,0:T(8,128)}, u32[]{:S(2)}, u32[]{:S(2)}) collective-permute-start(f32[6,24,384]{2,1,0:T(8,128)S(1)} %get-tuple-element.82), channel_id=1, source_target_pairs={{0,2},{4,6},{8,10},{12,14},{16,18},{20,22},{24,26},{28,30},{2,0},{... | collective-permute-start | bytes 663560 | tf_op jit(solution)/shard_map/cond/branch_1_fun/ppermute | solution.py:474
  36.5 9.7 %collective-permute-start.29 = (f32[6,24,384]{2,1,0:T(8,128)S(1)}, f32[6,24,384]{2,1,0:T(8,128)}, u32[]{:S(2)}, u32[]{:S(2)}) collective-permute-start(f32[6,24,384]{2,1,0:T(8,128)S(1)} %get-tuple-element.83), channel_id=1, source_target_pairs={{2,2},{6,30},{10,26},{14,22},{18,18},{22,14},{26,10},{30,6},{3,3},... | collective-permute-start | bytes 663560 | tf_op jit(solution)/shard_map/cond/branch_1_fun/ppermute | solution.py:474
  39.4 15.4 %collective-permute-start.28 = (f32[6,24,384]{2,1,0:T(8,128)S(1)}, f32[6,24,384]{2,1,0:T(8,128)}, u32[]{:S(2)}, u32[]{:S(2)}) collective-permute-start(f32[6,24,384]{2,1,0:T(8,128)S(1)} %get-tuple-element.83), channel_id=1, source_target_pairs={{2,6},{6,2},{10,30},{14,26},{18,22},{22,18},{26,14},{30,10},{3,7},... | collective-permute-start | bytes 663560 | tf_op jit(solution)/shard_map/cond/branch_1_fun/ppermute | solution.py:474

commit v2 on v1

--- a/solution.py
+++ b/solution.py
@@ -32,10 +32,19 @@
     return pltpu.roll(values, (-offset) % width, values.ndim - 1)
 
 
+def half_tiles(cols):
+    assert cols == 2 * LANES
+    return slice(0, LANES), slice(LANES, cols)
+
+
+def own_slot(packed, k, first):
+    return pltpu.roll(packed, lax.rem(first - SLOT * k + 2 * LANES, LANES), packed.ndim - 1)
+
+
 def four_slots(parts, source_lane, lane):
     packed = None
     for k, part in enumerate(parts):
-        moved = pltpu.roll(part, (SLOT * k - source_lane) % LANES, part.ndim - 1)
+        moved = pltpu.roll(part, lax.rem(SLOT * k - source_lane + LANES, LANES), part.ndim - 1)
         packed = moved if packed is None else jnp.where(lane >= SLOT * k, moved, packed)
     return packed
 
@@ -62,7 +71,23 @@
 
 
 def widen_kernel(
-    u, v, t, s, sea, zonal, merid, tally, from_west, from_east, fields, flat, msg_a, msg_b
+    top_lat,
+    seam,
+    u,
+    v,
+    t,
+    s,
+    sea,
+    zonal,
+    merid,
+    tally,
+    from_west,
+    from_east,
+    fields,
+    flat,
+    msg_a,
+    msg_b,
+    msg_c,
 ):
     levels, rows, cols = u.shape
     lane = lane_of((SUB, LANES))
@@ -95,26 +120,43 @@
         fill(msg_a, 0)
         fill(msg_b, rows - DEEP)
 
-
-def across_fold(near, far, offset, lane):
-    cols = near.shape[1] - LANES
-    count = cols // LANES
-    tiles = [far[:, cols:]] + [far[:, LANES * i : LANES * (i + 1)] for i in range(count)]
-    tiles += [near[:, LANES * i : LANES * (i + 1)] for i in range(count)] + [near[:, cols:]]
+    @pl.when(lax.axis_index("lat") == top_lat)
+    def _():
+        west, _ = fold_offset(seam, cols)
+        first = jnp.where(west, LANES - SLOT, 0)
+        for q in range(DEEP):
+            edges = []
+            for k in range(FIELDS):
+                low, high = (fields[k, rows - DEEP + q, :, at] for at in half_tiles(cols))
+                msg_c[k * DEEP + q] = jnp.where(west, high, low)
+                edges.append(jnp.where(west, low, high))
+            msg_c[FIELDS * DEEP + q] = four_slots(edges, first, lane)
+        low, high = (msg_b[FIELDS * DEEP, :, at] for at in half_tiles(cols))
+        msg_c[(FIELDS + 1) * DEEP] = jnp.where(west, high, low)
+        msg_c[(FIELDS + 1) * DEEP + 1] = jnp.where(west, low, high)
+
+
+def fold_offset(seam, cols):
+    rest = lax.rem(seam[0], cols)
+    return rest >= cols // 2, lax.rem(rest, LANES)
+
+
+def across_fold(line, rest, lane):
     back = LANES - 1 - lane
-    tiles = [jnp.take_along_axis(x, back, axis=1) for x in tiles[::-1]]
-    amount = cols + LANES - 1 - offset
-    tile, part = lax.div(amount, LANES), lax.rem(amount, LANES)
-    moved = []
-    for k in range(count + 3):
-        value = tiles[k]
-        for first in range(1, count):
-            value = jnp.where(tile == first + 1, tiles[k + first], value)
-        moved.append(pltpu.roll(value, LANES - part, 1))
+    part = LANES - 1 - rest
+    moved = [
+        pltpu.roll(jnp.take_along_axis(x, back, axis=1), LANES - part, 1) for x in line[::-1]
+    ]
     keep = lane < LANES - part
-    out = [jnp.where(keep, moved[k], moved[k + 1]) for k in range(count + 2)]
-    last = jnp.where(lane < SLOT, out[count + 1], jnp.where(lane >= LANES - SLOT, out[0], 0.0))
-    return jnp.concatenate(out[1 : count + 1] + [last], axis=1)
+    out = [jnp.where(keep, p, q) for p, q in zip(moved, moved[1:])]
+    last = jnp.where(lane < SLOT, out[-1], jnp.where(lane >= LANES - SLOT, out[0], 0.0))
+    return out[1:-1] + [last]
+
+
+def facing_line(west, whole, edge, half, half_edge):
+    from_west = [half_edge, half] + whole + [edge]
+    from_east = [edge] + whole + [half, half_edge]
+    return [jnp.where(west, p, q) for p, q in zip(from_west, from_east)]
 
 
 def weno_flux(speed, low2, low1, here, up1, up2, up3):
@@ -150,7 +192,32 @@
     return values
 
 
-def flux_kernel(
+def row_of(k, j, at, rows, fields, south, north):
+    if j < DEEP:
+        return south[k * DEEP + j, :, at]
+    if j < DEEP + rows:
+        return fields[k, j - DEEP, :, at]
+    return north[k * DEEP + j - DEEP - rows, :, at]
+
+
+def north_fluxes(index, first, tiles, rows, fields, south, north, speed_n, flux_n):
+    k, tile = lax.div(index, tiles), lax.rem(index, tiles)
+    at = pl.ds(pl.multiple_of(tile * LANES, LANES), LANES)
+    window = [row_of(first + k, j, at, rows, fields, south, north) for j in range(5)]
+    for j in range(rows + 1):
+        window.append(row_of(first + k, j + 5, at, rows, fields, south, north))
+        flux_n[k, j, :, at] = weno_flux(speed_n[j, :, at], *window)
+        window.pop(0)
+
+
+def row_rate(q, speed, rise, north_step):
+    flux = weno_flux(speed, *(wide_roll(q, i) if i else q for i in range(-2, 4)))
+    vertical = rise * (q + pltpu.roll(q, 1, 0))
+    below = pltpu.roll(vertical, SUB - 1, 0)
+    return -(flux - wide_roll(flux, -1)) - north_step - (vertical - below)
+
+
+def force_kernel(
     sizes,
     seam,
     fields,
@@ -158,22 +225,20 @@
     got_a,
     got_b,
     got_c,
-    tracer_t,
-    tracer_s,
     base_u,
     base_v,
     six,
     south,
     north,
-    wet,
     speed_n,
     speed_e,
+    rises,
+    wet,
     flux_n,
     press,
-    final,
 ):
     rows, lat_size = sizes
-    cols = tracer_t.shape[2]
+    cols = base_u.shape[2]
     width = cols + LANES
     lat = lax.axis_index("lat")
     even = lax.rem(lat, 2) == 0
@@ -196,24 +261,30 @@
 
     @pl.when(top)
     def _():
-        offset = lax.rem(seam[0], cols)
+        west, rest = fold_offset(seam, cols)
+        first = jnp.where(west, LANES - SLOT, 0)
+        tiles = [slice(LANES * i, LANES * (i + 1)) for i in range(width // LANES)]
+
+        def ghosts(plane, half, half_edge):
+            parts = [got_b[plane, :, at] for at in tiles]
+            line = facing_line(west, parts[:-1], parts[-1], half, half_edge)
+            return across_fold(line, rest, lane)
+
         for k in range(FIELDS):
             for q in range(DEEP):
-                ghost = across_fold(got_b[k * DEEP + q], got_c[k * DEEP + q], offset, lane)
-                north[k * DEEP + DEEP - 1 - q] = -ghost if k < 2 else ghost
-        ghost = across_fold(got_b[planes], got_c[planes], offset, lane)
-        north[planes, 0:1, :] = ghost[DEEP - 1 : DEEP, :]
-
-    def row_of(k, j, at):
-        if j < DEEP:
-            return south[k * DEEP + j, :, at]
-        if j < DEEP + rows:
-            return fields[k, j - DEEP, :, at]
-        return north[k * DEEP + j - DEEP - rows, :, at]
+                plane = k * DEEP + q
+                edge = own_slot(got_c[planes + q], k, first)
+                for at, ghost in zip(tiles, ghosts(plane, got_c[plane], edge)):
+                    north[k * DEEP + DEEP - 1 - q, :, at] = -ghost if k < 2 else ghost
+        for at, ghost in zip(tiles, ghosts(planes, got_c[planes + DEEP], got_c[planes + DEEP + 1])):
+            north[planes, 0:1, at] = ghost[DEEP - 1 : DEEP, :]
 
     level = lax.broadcasted_iota(jnp.int32, (SUB, width), 0)
     level_real = level.astype(jnp.float32)
     every = slice(None)
+
+    def row(k, j):
+        return row_of(k, j, every, rows, fields, south, north)
 
     def set_wet(index, tally_row):
         wet[index] = (level_real < jnp.broadcast_to(tally_row, (SUB, width))).astype(jnp.float32)
@@ -224,67 +295,72 @@
     set_wet(rows + 1, north[planes, 0:1, :])
 
     for j in range(rows + 1):
-        speed = row_of(1, j + 2, every) + row_of(1, j + 3, every)
-        speed_n[j] = 0.5 * speed * wet[j] * wet[j + 1]
+        speed_n[j] = 0.5 * (row(1, j + 2) + row(1, j + 3)) * wet[j] * wet[j + 1]
     for j in range(rows + 2):
-        density = 0.8 * row_of(3, j + 2, every) - 0.2 * row_of(2, j + 2, every)
+        density = 0.8 * row(3, j + 2) - 0.2 * row(2, j + 2)
         press[j] = level_sums(density, level, False) - 0.5 * density
 
-    def north_fluxes(index, carry):
-        k, tile = lax.div(index, width // LANES), lax.rem(index, width // LANES)
-        at = pl.ds(pl.multiple_of(tile * LANES, LANES), LANES)
-        window = [row_of(k, j, at) for j in range(5)]
-        for j in range(rows + 1):
-            window.append(row_of(k, j + 5, at))
-            flux_n[k, j, :, at] = weno_flux(speed_n[j, :, at], *window)
-            window.pop(0)
+    tiles = width // LANES
+
+    def northward(index, carry):
+        north_fluxes(index, 0, tiles, rows, fields, south, north, speed_n, flux_n)
         return carry
 
-    lax.fori_loop(0, FIELDS * (width // LANES), north_fluxes, 0)
-
+    lax.fori_loop(0, 2 * tiles, northward, 0)
     total_rows = rows * lat_size
 
     def one_row(j, carry):
         mask = wet[j + 1]
-        u = fields[0, j]
+        u, v = fields[0, j], fields[1, j]
         speed = 0.5 * (u + wide_roll(u, 1)) * mask * wide_roll(mask, 1)
         spread = speed - wide_roll(speed, -1) + (speed_n[j + 1] - speed_n[j])
         upward = -level_sums(spread, level, True)
         rise = jnp.where(level >= 1, (0.5 * COURANT) * upward, 0.0)
-        rates = []
-        for k in range(FIELDS):
-            q = fields[k, j]
-            flux = weno_flux(
-                speed,
-                wide_roll(q, -2),
-                wide_roll(q, -1),
-                q,
-                wide_roll(q, 1),
-                wide_roll(q, 2),
-                wide_roll(q, 3),
-            )
-            vertical = rise * (q + pltpu.roll(q, 1, 0))
-            below = pltpu.roll(vertical, SUB - 1, 0)
-            rates.append(
-                -(flux - wide_roll(flux, -1))
-                - (flux_n[k, j + 1] - flux_n[k, j])
-                - (vertical - below)
-            )
+        speed_e[j] = speed
+        rises[j] = rise
+        rate_u = row_rate(u, speed, rise, flux_n[0, j + 1] - flux_n[0, j])
+        rate_v = row_rate(v, speed, rise, flux_n[1, j + 1] - flux_n[1, j])
         place = (lat * rows + j).astype(jnp.float32)
         coriolis = CORIOLIS * (2.0 * (place + 0.5) / total_rows - 1.0)
-        v = fields[1, j]
         pressure = press[j + 1]
         grad_east = 0.5 * (wide_roll(pressure, 1) - wide_roll(pressure, -1))
         grad_north = 0.5 * (press[j + 2] - press[j])
-        force_u = rates[0] + coriolis * v - PRESSURE_GAIN * grad_east
-        force_v = rates[1] - coriolis * u - PRESSURE_GAIN * grad_north
+        force_u = rate_u + coriolis * v - PRESSURE_GAIN * grad_east
+        force_v = rate_v - coriolis * u - PRESSURE_GAIN * grad_north
         depth = jnp.maximum(flat[3, pl.ds(j, 1), :], 1.0)
         six[4, pl.ds(j, 1), :] = jnp.sum(mask * force_u, axis=0, keepdims=True) / depth
         six[5, pl.ds(j, 1), :] = jnp.sum(mask * force_v, axis=0, keepdims=True) / depth
         base_u[j] = (u + force_u)[:, :cols]
         base_v[j] = (v + force_v)[:, :cols]
-        for k in (2, 3):
-            final[k - 2, j] = (mask * (fields[k, j] + rates[k]))[:, :cols]
+        return carry
+
+    lax.fori_loop(0, rows, one_row, 0)
+    six[0:4] = flat[...]
+
+
+def tracer_kernel(
+    fields, flat, south, north, speed_n, speed_e, rises, tracer_t, tracer_s, flux_n, final
+):
+    rows = fields.shape[1]
+    cols = tracer_t.shape[2]
+    tiles = cols // LANES
+
+    def northward(index, carry):
+        north_fluxes(index, 2, tiles, rows, fields, south, north, speed_n, flux_n)
+        return carry
+
+    lax.fori_loop(0, 2 * tiles, northward, 0)
+    level = lax.broadcasted_iota(jnp.int32, (SUB, cols), 0).astype(jnp.float32)
+    aside = jnp.zeros((SUB, LANES), jnp.float32)
+
+    def one_row(j, carry):
+        tally = jnp.broadcast_to(flat[3, pl.ds(j, 1), pl.ds(0, cols)], (SUB, cols))
+        mask = (level < tally).astype(jnp.float32)
+        for k in (0, 1):
+            q = fields[2 + k, j]
+            step = jnp.concatenate([flux_n[k, j + 1] - flux_n[k, j], aside], axis=1)
+            rate = row_rate(q, speed_e[j], rises[j], step)
+            final[k, j] = mask * (q + rate)[:, :cols]
         return carry
 
     lax.fori_loop(0, rows, one_row, 0)
@@ -292,15 +368,18 @@
         row = slice(SUB * g, SUB * (g + 1))
         tracer_t[:, row, :] = jnp.swapaxes(final[0, row], 0, 1)
         tracer_s[:, row, :] = jnp.swapaxes(final[1, row], 0, 1)
-    six[0:4] = flat[...]
-
-
-def pair_kernel(sizes, six, got_a, msg_1, msg_2):
+
+
+def pair_kernel(sizes, seam, six, got_a, msg_1, full, full_low, half, half_low, *more):
     rows, lat_size = sizes
+    cols = six.shape[2] - LANES
     lat = lax.axis_index("lat")
     even = lax.rem(lat, 2) == 0
-    pair_even = lax.rem(lax.div(lat, 2), 2) == 0
+    pair = lax.div(lat, 2)
+    pair_even = lax.rem(pair, 2) == 0
+    top = pair == lat_size // 2 - 1
     rest = MARGIN - rows
+    lane = lane_of((SUB, LANES))
 
     def last(msg, lower, upper):
         msg[:, 0:rest, :] = lower[:, rows - rest : rows, :]
@@ -310,16 +389,47 @@
         msg[:, 0:rows, :] = lower[...]
         msg[:, rows:MARGIN, :] = upper[:, 0:rest, :]
 
+    def across(lower, upper, low):
+        whole_out, half_out = (full_low, half_low) if low else (full, half)
+        west, _ = fold_offset(seam, cols)
+        height = whole_out.shape[1]
+        count = six.shape[0]
+        for g in range(height // SUB):
+            up = 2 * rows - height + SUB * g
+            source, start = (lower, up) if up < rows else (upper, up - rows)
+            row, out = slice(start, start + SUB), slice(SUB * g, SUB * (g + 1))
+            edges, half_edges = [], []
+            for k in range(count):
+                left, right = (source[k, row, at] for at in half_tiles(cols))
+                whole_out[2 * k, out, :] = left
+                whole_out[2 * k + 1, out, :] = right
+                half_out[k, out, :] = jnp.where(west, right, left)
+                edges.append(source[k, row, cols:])
+                half_edges.append(jnp.where(west, left, right))
+            for i in range(0, count, 4):
+                packed = four_slots(edges[i : i + 4], jnp.where(west, 0, LANES - SLOT), lane)
+                whole_out[2 * count + i // 4, out, :] = packed
+                packed = four_slots(half_edges[i : i + 4], jnp.where(west, LANES - SLOT, 0), lane)
+                half_out[count + i // 4, out, :] = packed
+
     for bottom, lower, upper in ((True, six, got_a), (False, got_a, six)):
-        for which in (True, False):
-            here = (even if bottom else jnp.logical_not(even)) & (
-                pair_even if which else jnp.logical_not(pair_even)
-            )
-
-            @pl.when(here)
-            def _(lower=lower, upper=upper, which=which):
-                (last if which else first)(msg_1, lower, upper)
-                (first if which else last)(msg_2, lower, upper)
+        mine = even if bottom else jnp.logical_not(even)
+
+        @pl.when(mine & pair_even)
+        def _(lower=lower, upper=upper):
+            last(msg_1, lower, upper)
+            if more:
+                first(more[0], lower, upper)
+
+        @pl.when(mine & jnp.logical_not(pair_even))
+        def _(lower=lower, upper=upper):
+            first(msg_1, lower, upper)
+            if more:
+                last(more[0], lower, upper)
+
+        @pl.when(mine & top)
+        def _(lower=lower, upper=upper, bottom=bottom):
+            across(lower, upper, bottom)
 
 
 def wave_kernel(
@@ -328,18 +438,17 @@
     six,
     got_a,
     got_1,
-    got_2,
-    got_f,
+    full,
+    full_low,
+    half,
+    half_low,
     base_u,
     base_v,
-    out_u,
-    out_v,
-    out_sea,
-    out_zonal,
-    out_merid,
-    space,
+    *rest,
 ):
     rows, levels, lat_size = sizes
+    got_2 = rest[:-6]
+    out_u, out_v, out_sea, out_zonal, out_merid, space = rest[-6:]
     cols = out_sea.shape[1]
     width = cols + LANES
     lat = lax.axis_index("lat")
@@ -364,29 +473,43 @@
 
     @pl.when(pair_even)
     def _():
-        space[:, below, :] = got_2[...]
+        space[:, below, :] = got_2[0][...] if got_2 else jnp.zeros_like(got_1)
         space[:, above, :] = got_1[...]
 
     @pl.when(jnp.logical_not(pair_even))
     def _():
         space[:, below, :] = got_1[...]
 
-    @pl.when(jnp.logical_not(pair_even) & jnp.logical_not(top))
-    def _():
-        space[:, above, :] = got_2[...]
-
-    @pl.when(top)
-    def _():
-        offset = lax.rem(seam[0], cols)
+    if got_2:
+
+        @pl.when(jnp.logical_not(pair_even) & jnp.logical_not(top))
+        def _():
+            space[:, above, :] = got_2[0][...]
+
+    def ghosts(whole, part):
+        west, rest = fold_offset(seam, cols)
         turn = SUB - 1 - lax.broadcasted_iota(jnp.int32, (SUB, LANES), 0)
+        count = six.shape[0]
+        height = whole.shape[1]
         for k, parity in enumerate((1.0, -1.0, -1.0, 1.0, -1.0, -1.0)):
-            for g in range(MARGIN // SUB):
+            for g in range(height // SUB):
                 row = slice(SUB * g, SUB * (g + 1))
-                ghost = across_fold(got_2[k, row, :], got_f[k, row, :], offset, lane)
-                place = above.start + MARGIN - SUB * (g + 1)
-                for i in range(width // LANES):
-                    part = jnp.take_along_axis(ghost[:, LANES * i : LANES * (i + 1)], turn, axis=0)
-                    space[k, place : place + SUB, LANES * i : LANES * (i + 1)] = parity * part
+                edge = own_slot(whole[2 * count + k // 4, row, :], k % 4, jnp.where(west, 0, LANES - SLOT))
+                half_edge = own_slot(part[count + k // 4, row, :], k % 4, jnp.where(west, LANES - SLOT, 0))
+                tiles = [whole[2 * k, row, :], whole[2 * k + 1, row, :]]
+                line = facing_line(west, tiles, edge, part[k, row, :], half_edge)
+                place = above.start + height - SUB * (g + 1)
+                for i, ghost in enumerate(across_fold(line, rest, lane)):
+                    ghost = parity * jnp.take_along_axis(ghost, turn, axis=0)
+                    space[k, place : place + SUB, LANES * i : LANES * (i + 1)] = ghost
+
+    @pl.when(top & jnp.logical_not(even))
+    def _():
+        ghosts(full, half)
+
+    @pl.when(top & even)
+    def _():
+        ghosts(full_low, half_low)
 
     height = rows + 2 * MARGIN
     window = pl.ds(pl.multiple_of(jnp.where(even, 0, rows), SUB), height)
@@ -463,6 +586,11 @@
     width = cols + LANES
     assert levels == SUB and rows % SUB == 0 and lat_size % 4 == 0
     tile = lax.rem(lax.div(seam[0], cols) + lax.axis_index("lon"), lon_size)
+    choice = 2 * tile + (lax.rem(seam[0], cols) >= cols // 2).astype(jnp.int32)
+
+    def partners(chosen):
+        turn, west = divmod(chosen, 2)
+        return (turn, turn - 1) if west else (turn - 1, turn)
 
     def moves(lats, fold=(), turn=0):
         pairs = [(x * lat_size + a, x * lat_size + b) for a, b in lats for x in range(lon_size)]
@@ -482,7 +610,7 @@
     chips = lat_size // 2
     chips_1 = both((2 * c + b, 2 * c + 2 + b) for c in range(0, chips - 1, 2) for b in (0, 1))
     chips_2 = both((2 * c + b, 2 * c + 2 + b) for c in range(1, chips - 1, 2) for b in (0, 1))
-    last, last_two = (lat_size - 1,), (lat_size - 2, lat_size - 1)
+    high, low = (lat_size - 1,), (lat_size - 2,)
 
     message = real(levels + 1, rows, LANES)
     flat_args = (u, v, t, s, sea, zonal, merid, tally)
@@ -491,63 +619,89 @@
     from_east = lax.ppermute(west, "lon", [(b, a) for a, b in ring])
 
     deep = real(FIELDS * DEEP + 1, SUB, width)
-    fields, flat, msg_a, msg_b = call(
-        widen_kernel,
-        (real(FIELDS, rows, SUB, width), real(FIELDS, rows, width), deep, deep),
-    )(*flat_args, from_west, from_east)
-
-    def deep_exchange(turn):
-        def run(a, b):
+    fields, flat, msg_a, msg_b, msg_c = call(
+        functools.partial(widen_kernel, lat_size - 1),
+        (
+            real(FIELDS, rows, SUB, width),
+            real(FIELDS, rows, width),
+            deep,
+            deep,
+            real((FIELDS + 1) * DEEP + 2, SUB, LANES),
+        ),
+        seam=True,
+    )(seam, *flat_args, from_west, from_east)
+
+    def deep_exchange(chosen):
+        whole, half = partners(chosen)
+
+        def run(a, b, c):
             return (
                 send(a, moves(inside)),
-                send(b, moves(between, last, turn)),
-                send(b, moves((), last, turn - 1)),
+                send(b, moves(between, high, whole)),
+                send(c, moves((), high, half)),
             )
 
         return run
 
-    got_a, got_b, got_c = lax.switch(tile, [deep_exchange(i) for i in range(lon_size)], msg_a, msg_b)
+    branches = range(2 * lon_size)
+    got_a, got_b, got_c = lax.switch(
+        choice, [deep_exchange(i) for i in branches], msg_a, msg_b, msg_c
+    )
 
     base = real(rows, SUB, cols)
     tracer = real(levels, rows, cols)
-    tracer_t, tracer_s, base_u, base_v, six = call(
-        functools.partial(flux_kernel, (rows, lat_size)),
-        (tracer, tracer, base, base, real(6, rows, width)),
-        scratch=(
-            deep.shape,
-            deep.shape,
-            (rows + 2, SUB, width),
-            (rows + 1, SUB, width),
-            (rows, SUB, width),
-            (FIELDS, rows + 1, SUB, width),
-            (rows + 2, SUB, width),
-            (2, rows, SUB, cols),
-        ),
+    wide = real(rows, SUB, width)
+    base_u, base_v, six, south, north, speed_n, speed_e, rises = call(
+        functools.partial(force_kernel, (rows, lat_size)),
+        (base, base, real(6, rows, width), deep, deep, real(rows + 1, SUB, width), wide, wide),
+        scratch=((rows + 2, SUB, width), (2, rows + 1, SUB, width), (rows + 2, SUB, width)),
         seam=True,
     )(seam, fields, flat, got_a, got_b, got_c)
 
     got_pair = send(six, moves(inside))
-    strip = real(6, MARGIN, width)
-    msg_1, msg_2 = call(functools.partial(pair_kernel, (rows, lat_size)), (strip, strip))(six, got_pair)
-
-    def strip_exchange(turn):
-        def run(a, b):
-            return (
-                send(a, moves(chips_1)),
-                send(b, moves(chips_2, last_two, turn)),
-                send(b, moves((), last_two, turn - 1)),
-            )
+    count = six.shape[0]
+    packs = -(-count // 4)
+    strip = real(count, MARGIN, width)
+    rest = MARGIN - rows
+    strips = (strip,) + tuple(
+        real(planes, height, LANES)
+        for planes in (2 * count + packs, count + packs)
+        for height in (MARGIN, rest)
+    )
+    strips += (strip,) * bool(chips_2)
+    messages = call(functools.partial(pair_kernel, (rows, lat_size)), strips, seam=True)(
+        seam, six, got_pair
+    )
+    tracers = call(
+        tracer_kernel,
+        (tracer, tracer),
+        scratch=((2, rows + 1, SUB, cols), (2, rows, SUB, cols)),
+    )
+
+    def strip_exchange(chosen):
+        whole, half = partners(chosen)
+        routes = [moves(chips_1)]
+        routes += [moves((), at, turn) for turn in (whole, half) for at in (high, low)]
+        routes += [moves(chips_2)] * bool(chips_2)
+
+        def run(messages, inputs):
+            return [send(m, pairs) for m, pairs in zip(messages, routes)], tracers(*inputs)
 
         return run
 
-    got_1, got_2, got_f = lax.switch(tile, [strip_exchange(i) for i in range(lon_size)], msg_1, msg_2)
+    received, (tracer_t, tracer_s) = lax.switch(
+        choice,
+        [strip_exchange(i) for i in branches],
+        messages,
+        (fields, flat, south, north, speed_n, speed_e, rises),
+    )
     plane = real(rows, cols)
     out_u, out_v, out_sea, out_zonal, out_merid = call(
         functools.partial(wave_kernel, (rows, levels, lat_size)),
         (tracer, tracer, plane, plane, plane),
-        scratch=((6, 2 * rows + 2 * MARGIN, width),),
+        scratch=((count, 2 * rows + 2 * MARGIN, width),),
         seam=True,
-    )(seam, six, got_pair, got_1, got_2, got_f, base_u, base_v)
+    )(seam, six, got_pair, *received[:5], base_u, base_v, *received[5:])
     return out_u, out_v, tracer_t, tracer_s, out_sea, out_zonal, out_merid
 
 

time: 60.6 us -> 55.7 us (0.919)
  the two profiles are of different devices: /device:TPU:27 before, /device:TPU:3 now
where the time goes in v2:
time: 55.7 us; the launch traced here: 56.6 us
  Pallas kernels  23.3 us (42%)
  starting transfers between devices  20.4 us (37%)
  waiting for transfers between devices  6.63 us (12%)
  local copies, waits for them, and re-layouts  3.09 us (6%)
  between operations  2.65 us (5%)
  loops' own time  0.56 us (1%)
    pallas_call x6, Pallas kernels, run(): pl.pallas_call(kernel, out_shape=outs, in_specs=specs, out_specs=jax.tree...  23.3 us
    ppermute x9, starting transfers between devices, send(): return lax.ppermute(values, ('lon', 'lat'), pairs)  16.2 us
    ppermute x9, waiting for transfers between devices, send(): return lax.ppermute(values, ('lon', 'lat'), pairs)  6.63 us
    ppermute x1, starting transfers between devices, on_device(): from_east = lax.ppermute(west, 'lon', [(b, a) for a, b in ring])  3.04 us
    unnamed x8, local copies, waits for them, and re-layouts  2.57 us
    ppermute x1, starting transfers between devices, on_device(): from_west = lax.ppermute(east, 'lon', ring)  1.24 us
  transfers between devices with their start and end apart: 11, of which 2 were waited for; matrix products, arithmetic and copies ran while one was open for 1% of the time, Pallas kernels for 8%

profile of v2, /device:TPU:3, one launch (start us, length us, event | category | flops | bytes accessed | tf_op | source)
XLA Modules:
  0.0 56.6 jit_solution(9565308789165550717)
XLA Ops:
  0.6 1.9 %shard_map.144 = (f32[9,16,128]{2,1,0:T(8,128)}, f32[9,16,128]{2,1,0:T(8,128)}) custom-call(f32[8,16,256]{2,1,0:T(8,128)} %u.3, f32[8,16,256]{2,1,0:T(8,128)} %v.3, f32[8,16,256]{2,1,0:T(8,128)} %t.3, f32[8,16,256]{2,1,0:T(8,128)} %s.3, f32[16,256]{1,0:T(8,128)} %sea.3, f32[16,256]{1,0:T(8,128)} %zonal.3, f32[16,256]{1,0:T(8,128)} %merid.3, s32[16,256]{1,0:T(8,128)} %tally.3), custom_call_target="tpu_custom_call" | custom-call | tf_op jit(solution)/shard_map/pallas_call | solution.py:572
  2.6 1.2 %collective-permute-start.128 = (f32[9,16,128]{2,1,0:T(8,128)}, f32[9,16,128]{2,1,0:T(8,128)S(1)}, u32[]{:S(2)}, u32[]{:S(2)}) collective-permute-start(f32[9,16,128]{2,1,0:T(8,128)} %get-tuple-element.794), channel_id=1, source_target_pairs={{0,4},{4,8},{8,12},{12,16},{16,20},{20,24},{24,28},{28,0},{1,5},{5... | collective-permute-start | bytes 221192 | tf_op jit(solution)/shard_map/ppermute | solution.py:618
  3.8 3.0 %collective-permute-start.129 = (f32[9,16,128]{2,1,0:T(8,128)}, f32[9,16,128]{2,1,0:T(8,128)S(1)}, u32[]{:S(2)}, u32[]{:S(2)}) collective-permute-start(f32[9,16,128]{2,1,0:T(8,128)} %get-tuple-element.795), channel_id=1, source_target_pairs={{4,0},{8,4},{12,8},{16,12},{20,16},{24,20},{28,24},{0,28},{5,1},{9... | collective-permute-start | bytes 221192 | tf_op jit(solution)/shard_map/ppermute | solution.py:619
  6.9 0.7 %copy-done.3 = s32[256]{0:T(256)S(1)} copy-done((s32[256]{0:T(256)S(1)}, s32[256]{0:T(256)}, u32[]{:S(2)}) %copy-start.3) | copy-done | bytes 1048
  7.5 0.5 slice.4
  10.0 0.0 collective-permute-done.128.from_west
  10.0 0.0 copy-start.1
  10.0 0.6 %copy-done.1 = f32[9,16,128]{2,1,0:T(8,128)} copy-done((f32[9,16,128]{2,1,0:T(8,128)}, f32[9,16,128]{2,1,0:T(8,128)S(1)}, u32[]{:S(2)}) %copy-start.1) | copy-done | bytes 73752
  10.7 0.6 %copy-done.2 = f32[9,16,128]{2,1,0:T(8,128)} copy-done((f32[9,16,128]{2,1,0:T(8,128)}, f32[9,16,128]{2,1,0:T(8,128)S(1)}, u32[]{:S(2)}) %copy-start.2) | copy-done | bytes 73752
  11.3 1.6 %shard_map.145 = (f32[4,16,8,384]{3,2,1,0:T(8,128)S(1)}, f32[4,16,384]{2,1,0:T(8,128)S(1)}, f32[13,8,384]{2,1,0:T(8,128)S(1)}, f32[13,8,384]{2,1,0:T(8,128)S(1)}, f32[17,8,128]{2,1,0:T(8,128)S(1)}) custom-call(s32[256]{0:T(256)} %seam.7, f32[8,16,256]{2,1,0:T(8,128)} %u.3, f32[8,16,256]{2,1,0:T(8,128)} %v.3, f32[8,16,256]{2,1,0:T(8,128)} %t.3, ...), custom_call_target="tpu_custom_call" | custom-call | tf_op jit(solution)/shard_map/pallas_call | solution.py:572
  12.9 13.2 %conditional.2 = (f32[13,8,384]{2,1,0:T(8,128)}, f32[13,8,384]{2,1,0:T(8,128)}, f32[17,8,128]{2,1,0:T(8,128)}) conditional(s32[]{:T(128)} %clamp.4, (f32[13,8,384]{2,1,0:T(8,128)S(1)}, f32[13,8,384]{2,1,0:T(8,128)S(1)}, f32[17,8,128]{2,1,0:T(8,128)S(1)}) %tuple.136, (f32[13,8,384]{2,1,0:T(8,128)S(1)}, ...), branch_computations={%region_0.0_spmd, %region_1.0_spmd, %region_2.0_spmd, %region_3.0_... | conditional | bytes 1556624 | solution.py:647
  12.9 1.1 %collective-permute-start.45 = (f32[13,8,384]{2,1,0:T(8,128)S(1)}, f32[13,8,384]{2,1,0:T(8,128)}, u32[]{:S(2)}, u32[]{:S(2)}) collective-permute-start(f32[13,8,384]{2,1,0:T(8,128)S(1)} %get-tuple-element.525), channel_id=1, source_target_pairs={{0,1},{4,5},{8,9},{12,13},{16,17},{20,21},{24,25},{28,29},{1,0},{5... | collective-permute-start | bytes 479240 | tf_op jit(solution)/shard_map/cond/branch_15_fun/ppermute | solution.py:602
  14.0 5.1 %collective-permute-start.46 = (f32[13,8,384]{2,1,0:T(8,128)S(1)}, f32[13,8,384]{2,1,0:T(8,128)}, u32[]{:S(2)}, u32[]{:S(2)}) collective-permute-start(f32[13,8,384]{2,1,0:T(8,128)S(1)} %get-tuple-element.526), channel_id=1, source_target_pairs={{1,2},{5,6},{9,10},{13,14},{17,18},{21,22},{25,26},{29,30},{2,1},{... | collective-permute-start | bytes 479240 | tf_op jit(solution)/shard_map/cond/branch_15_fun/ppermute | solution.py:602
  19.1 1.9 %collective-permute-start.47 = (f32[17,8,128]{2,1,0:T(8,128)S(1)}, f32[17,8,128]{2,1,0:T(8,128)}, u32[]{:S(2)}, u32[]{:S(2)}) collective-permute-start(f32[17,8,128]{2,1,0:T(8,128)S(1)} %get-tuple-element.527), channel_id=1, source_target_pairs={{3,27},{7,23},{11,19},{15,15},{19,11},{23,7},{27,3},{31,31}} | collective-permute-start | bytes 208904 | tf_op jit(solution)/shard_map/cond/branch_15_fun/ppermute | solution.py:602
  21.1 5.0 %collective-permute-done.47 = f32[17,8,128]{2,1,0:T(8,128)} collective-permute-done((f32[17,8,128]{2,1,0:T(8,128)S(1)}, f32[17,8,128]{2,1,0:T(8,128)}, u32[]{:S(2)}, u32[]{:S(2)}) %collective-permute-start.47) | collective-permute-done | bytes 69664 | tf_op jit(solution)/shard_map/cond/branch_15_fun/ppermute | solution.py:602
  26.1 0.0 collective-permute-done.45
  26.1 0.0 collective-permute-done.46
  26.1 6.9 %shard_map.146 = (f32[16,8,256]{2,1,0:T(8,128)}, f32[16,8,256]{2,1,0:T(8,128)}, f32[6,16,384]{2,1,0:T(8,128)}, f32[13,8,384]{2,1,0:T(8,128)S(1)}, f32[13,8,384]{...) custom-call(s32[256]{0:T(256)} %seam.7, ...), custom_call_target="tpu_custom_call" | custom-call | tf_op jit(solution)/shard_map/pallas_call | solution.py:572
  32.9 0.0 collective-permute-start.130
  33.0 1.6 %collective-permute-done.130.got_a = f32[6,16,384]{2,1,0:T(8,128)S(1)} collective-permute-done((f32[6,16,384]{2,1,0:T(8,128)}, f32[6,16,384]{2,1,0:T(8,128)S(1)}, u32[]{:S(2)}, u32[]{:S(2)}) %collective-permute-start.130) | collective-permute-done | bytes 147488 | tf_op jit(solution)/shard_map/ppermute | solution.py:602
  34.5 0.6 %copy-done = f32[6,16,384]{2,1,0:T(8,128)} copy-done((f32[6,16,384]{2,1,0:T(8,128)}, f32[6,16,384]{2,1,0:T(8,128)S(1)}, u32[]{:S(2)}) %copy-start) | copy-done | bytes 147480
  35.2 1.2 %shard_map.147 = (f32[6,24,384]{2,1,0:T(8,128)S(1)}, f32[14,24,128]{2,1,0:T(8,128)S(1)}, f32[14,8,128]{2,1,0:T(8,128)S(1)}, f32[8,24,128]{2,1,0:T(8,128)S(1)}, f32[8,8,128]{2,1,0:T(8,128)S(1)}) custom-call(s32[256]{0:T(256)} %seam.7, f32[6,16,384]{2,1,0:T(8,128)} %get-tuple-element.804.six, f32[6,16,384]{2,1,0:T(8,128)} %copy-done), custom_call_target="tpu_custom_call" | custom-call | tf_op jit(solution)/shard_map/pallas_call | solution.py:572
  36.3 13.2 %conditional.3 = (f32[6,24,384]{2,1,0:T(8,128)}, f32[14,24,128]{2,1,0:T(8,128)}, f32[14,8,128]{2,1,0:T(8,128)}, f32[8,24,128]{2,1,0:T(8,128)}, f32[8,8,128]{2,1,...) conditional(s32[]{:T(128)} %clamp.4, (f32[6,24,384]{2,1,0:T(8,128)S(1)}, ...), branch_computations={%region_16.0_spmd, %region_17.0_spmd, %region_18.0_spmd, %region_1... | conditional | bytes 2326784 | solution.py:692
  36.6 0.1 collective-permute-start.123
  36.7 1.9 %collective-permute-start.124 = (f32[14,24,128]{2,1,0:T(8,128)S(1)}, f32[14,24,128]{2,1,0:T(8,128)}, u32[]{:S(2)}, u32[]{:S(2)}) collective-permute-start(f32[14,24,128]{2,1,0:T(8,128)S(1)} %get-tuple-element.739), channel_id=1, source_target_pairs={{3,31},{7,27},{11,23},{15,19},{19,15},{23,11},{27,7},{31,3}} | collective-permute-start | bytes 516104 | tf_op jit(solution)/shard_map/cond/branch_15_fun/ppermute | solution.py:602
  38.6 3.5 %collective-permute-start.126 = (f32[8,24,128]{2,1,0:T(8,128)S(1)}, f32[8,24,128]{2,1,0:T(8,128)}, u32[]{:S(2)}, u32[]{:S(2)}) collective-permute-start(f32[8,24,128]{2,1,0:T(8,128)S(1)} %get-tuple-element.741), channel_id=1, source_target_pairs={{3,27},{7,23},{11,19},{15,15},{19,11},{23,7},{27,3},{31,31}} | collective-permute-start | bytes 294920 | tf_op jit(solution)/shard_map/cond/branch_15_fun/ppermute | solution.py:602
  42.1 1.3 %collective-permute-start.125 = (f32[14,8,128]{2,1,0:T(8,128)S(1)}, f32[14,8,128]{2,1,0:T(8,128)}, u32[]{:S(2)}, u32[]{:S(2)}) collective-permute-start(f32[14,8,128]{2,1,0:T(8,128)S(1)} %get-tuple-element.740), channel_id=1, source_target_pairs={{2,30},{6,26},{10,22},{14,18},{18,14},{22,10},{26,6},{30,2}} | collective-permute-start | bytes 172040 | tf_op jit(solution)/shard_map/cond/branch_15_fun/ppermute | solution.py:602
  43.4 1.3 %collective-permute-start.127 = (f32[8,8,128]{2,1,0:T(8,128)S(1)}, f32[8,8,128]{2,1,0:T(8,128)}, u32[]{:S(2)}, u32[]{:S(2)}) collective-permute-start(f32[8,8,128]{2,1,0:T(8,128)S(1)} %get-tuple-element.742), channel_id=1, source_target_pairs={{2,26},{6,22},{10,18},{14,14},{18,10},{22,6},{26,2},{30,30}} | collective-permute-start | bytes 98312 | tf_op jit(solution)/shard_map/cond/branch_15_fun/ppermute | solution.py:602
  44.7 4.7 %branch_15_fun.1 = (f32[8,16,256]{2,1,0:T(8,128)}, f32[8,16,256]{2,1,0:T(8,128)}) custom-call(f32[4,16,8,384]{3,2,1,0:T(8,128)S(1)} %get-tuple-element.743.fields, f32[4,16,384]{2,1,0:T(8,128)S(1)} %get-tuple-element.744.flat, f32[13,8,384]{2,1,0:T(8,128)S(1)} %get-tuple-element.745.south, f32[13,8,384]{2,1,0:T(8,128)S(1)} %get-tuple-element.746.north, ...), custom_call_target="tpu_custom_call" | custom-call | tf_op jit(solution)/shard_map/cond/branch_15_fun/pallas_call | solution.py:572
  49.3 0.0 collective-permute-done.127
  49.3 0.0 collective-permute-done.124
  49.6 7.1 %shard_map.148 = (f32[8,16,256]{2,1,0:T(8,128)}, f32[8,16,256]{2,1,0:T(8,128)}, f32[16,256]{1,0:T(8,128)}, f32[16,256]{1,0:T(8,128)}, f32[16,256]{1,0:T(8,128)}) custom-call(s32[256]{0:T(256)} %seam.7, f32[6,16,384]{2,1,0:T(8,128)} %get-tuple-element.804.six, f32[6,16,384]{2,1,0:T(8,128)} %copy-done, f32[6,24,384]{2,1,0:T(8,128)} %get-tuple-element.815.got_1, ...), custom_call_target="tpu_custom_call" | custom-call | tf_op jit(solution)/shard_map/pallas_call | solution.py:572
  (7 shorter events, 0.0 us)
Async XLA Ops:
  2.6 7.4 %collective-permute-start.128 = (f32[9,16,128]{2,1,0:T(8,128)}, f32[9,16,128]{2,1,0:T(8,128)S(1)}, u32[]{:S(2)}, u32[]{:S(2)}) collective-permute-start(f32[9,16,128]{2,1,0:T(8,128)} %get-tuple-element.794), channel_id=1, source_target_pairs={{0,4},{4,8},{8,12},{12,16},{16,20},{20,24},{24,28},{28,0},{1,5},{5... | collective-permute-start | bytes 221192 | tf_op jit(solution)/shard_map/ppermute | solution.py:618
  3.8 6.2 %collective-permute-start.129 = (f32[9,16,128]{2,1,0:T(8,128)}, f32[9,16,128]{2,1,0:T(8,128)S(1)}, u32[]{:S(2)}, u32[]{:S(2)}) collective-permute-start(f32[9,16,128]{2,1,0:T(8,128)} %get-tuple-element.795), channel_id=1, source_target_pairs={{4,0},{8,4},{12,8},{16,12},{20,16},{24,20},{28,24},{0,28},{5,1},{9... | collective-permute-start | bytes 221192 | tf_op jit(solution)/shard_map/ppermute | solution.py:619
  6.9 0.7 %copy-start.3 = (s32[256]{0:T(256)S(1)}, s32[256]{0:T(256)}, u32[]{:S(2)}) copy-start(s32[256]{0:T(256)} %seam.7) | copy-start | bytes 3076
  10.0 0.6 %copy-start.1 = (f32[9,16,128]{2,1,0:T(8,128)}, f32[9,16,128]{2,1,0:T(8,128)S(1)}, u32[]{:S(2)}) copy-start(f32[9,16,128]{2,1,0:T(8,128)S(1)} %collective-permute-done.128.from_west) | copy-start | bytes 221188
  10.7 0.6 %copy-start.2 = (f32[9,16,128]{2,1,0:T(8,128)}, f32[9,16,128]{2,1,0:T(8,128)S(1)}, u32[]{:S(2)}) copy-start(f32[9,16,128]{2,1,0:T(8,128)S(1)} %collective-permute-done.129.from_east) | copy-start | bytes 221188
  12.9 13.2 %collective-permute-start.45 = (f32[13,8,384]{2,1,0:T(8,128)S(1)}, f32[13,8,384]{2,1,0:T(8,128)}, u32[]{:S(2)}, u32[]{:S(2)}) collective-permute-start(f32[13,8,384]{2,1,0:T(8,128)S(1)} %get-tuple-element.525), channel_id=1, source_target_pairs={{0,1},{4,5},{8,9},{12,13},{16,17},{20,21},{24,25},{28,29},{1,0},{5... | collective-permute-start | bytes 479240 | tf_op jit(solution)/shard_map/cond/branch_15_fun/ppermute | solution.py:602
  14.0 12.0 %collective-permute-start.46 = (f32[13,8,384]{2,1,0:T(8,128)S(1)}, f32[13,8,384]{2,1,0:T(8,128)}, u32[]{:S(2)}, u32[]{:S(2)}) collective-permute-start(f32[13,8,384]{2,1,0:T(8,128)S(1)} %get-tuple-element.526), channel_id=1, source_target_pairs={{1,2},{5,6},{9,10},{13,14},{17,18},{21,22},{25,26},{29,30},{2,1},{... | collective-permute-start | bytes 479240 | tf_op jit(solution)/shard_map/cond/branch_15_fun/ppermute | solution.py:602
  19.1 7.0 %collective-permute-start.47 = (f32[17,8,128]{2,1,0:T(8,128)S(1)}, f32[17,8,128]{2,1,0:T(8,128)}, u32[]{:S(2)}, u32[]{:S(2)}) collective-permute-start(f32[17,8,128]{2,1,0:T(8,128)S(1)} %get-tuple-element.527), channel_id=1, source_target_pairs={{3,27},{7,23},{11,19},{15,15},{19,11},{23,7},{27,3},{31,31}} | collective-permute-start | bytes 208904 | tf_op jit(solution)/shard_map/cond/branch_15_fun/ppermute | solution.py:602
  32.9 1.6 %collective-permute-start.130 = (f32[6,16,384]{2,1,0:T(8,128)}, f32[6,16,384]{2,1,0:T(8,128)S(1)}, u32[]{:S(2)}, u32[]{:S(2)}) collective-permute-start(f32[6,16,384]{2,1,0:T(8,128)} %get-tuple-element.804.six), channel_id=1, source_target_pairs={{0,1},{4,5},{8,9},{12,13},{16,17},{20,21},{24,25},{28,29},{1,0},{5... | collective-permute-start | bytes 442376 | tf_op jit(solution)/shard_map/ppermute | solution.py:602
  34.5 0.6 %copy-start = (f32[6,16,384]{2,1,0:T(8,128)}, f32[6,16,384]{2,1,0:T(8,128)S(1)}, u32[]{:S(2)}) copy-start(f32[6,16,384]{2,1,0:T(8,128)S(1)} %collective-permute-done.130.got_a) | copy-start | bytes 442372
  36.6 12.8 %collective-permute-start.123 = (f32[6,24,384]{2,1,0:T(8,128)S(1)}, f32[6,24,384]{2,1,0:T(8,128)}, u32[]{:S(2)}, u32[]{:S(2)}) collective-permute-start(f32[6,24,384]{2,1,0:T(8,128)S(1)} %get-tuple-element.738), channel_id=1, source_target_pairs={{0,2},{4,6},{8,10},{12,14},{16,18},{20,22},{24,26},{28,30},{2,0},{... | collective-permute-start | bytes 663560 | tf_op jit(solution)/shard_map/cond/branch_15_fun/ppermute | solution.py:602
  36.7 12.7 %collective-permute-start.124 = (f32[14,24,128]{2,1,0:T(8,128)S(1)}, f32[14,24,128]{2,1,0:T(8,128)}, u32[]{:S(2)}, u32[]{:S(2)}) collective-permute-start(f32[14,24,128]{2,1,0:T(8,128)S(1)} %get-tuple-element.739), channel_id=1, source_target_pairs={{3,31},{7,27},{11,23},{15,19},{19,15},{23,11},{27,7},{31,3}} | collective-permute-start | bytes 516104 | tf_op jit(solution)/shard_map/cond/branch_15_fun/ppermute | solution.py:602
  38.6 10.7 %collective-permute-start.126 = (f32[8,24,128]{2,1,0:T(8,128)S(1)}, f32[8,24,128]{2,1,0:T(8,128)}, u32[]{:S(2)}, u32[]{:S(2)}) collective-permute-start(f32[8,24,128]{2,1,0:T(8,128)S(1)} %get-tuple-element.741), channel_id=1, source_target_pairs={{3,27},{7,23},{11,19},{15,15},{19,11},{23,7},{27,3},{31,31}} | collective-permute-start | bytes 294920 | tf_op jit(solution)/shard_map/cond/branch_15_fun/ppermute | solution.py:602
  42.1 7.2 %collective-permute-start.125 = (f32[14,8,128]{2,1,0:T(8,128)S(1)}, f32[14,8,128]{2,1,0:T(8,128)}, u32[]{:S(2)}, u32[]{:S(2)}) collective-permute-start(f32[14,8,128]{2,1,0:T(8,128)S(1)} %get-tuple-element.740), channel_id=1, source_target_pairs={{2,30},{6,26},{10,22},{14,18},{18,14},{22,10},{26,6},{30,2}} | collective-permute-start | bytes 172040 | tf_op jit(solution)/shard_map/cond/branch_15_fun/ppermute | solution.py:602
  43.4 5.9 %collective-permute-start.127 = (f32[8,8,128]{2,1,0:T(8,128)S(1)}, f32[8,8,128]{2,1,0:T(8,128)}, u32[]{:S(2)}, u32[]{:S(2)}) collective-permute-start(f32[8,8,128]{2,1,0:T(8,128)S(1)} %get-tuple-element.742), channel_id=1, source_target_pairs={{2,26},{6,22},{10,18},{14,14},{18,10},{22,6},{26,2},{30,30}} | collective-permute-start | bytes 98312 | tf_op jit(solution)/shard_map/cond/branch_15_fun/ppermute | solution.py:602

commit v3 on v2

--- a/solution.py
+++ b/solution.py
@@ -21,6 +21,7 @@
 DEEP = 3
 FIELDS = 4
 MARGIN = 2 * SUBSTEPS
+GRANT = 16 << 20
 
 
 def lane_of(shape):
@@ -52,16 +53,29 @@
 def pack_kernel(u, v, t, s, sea, zonal, merid, tally, east, west):
     levels, rows, cols = u.shape
     lane = lane_of((SUB, LANES))
-    lo, hi = slice(0, LANES), slice(cols - LANES, cols)
-    for g in range(rows // SUB):
-        row = slice(SUB * g, SUB * (g + 1))
-        for out, where, first in ((east, hi, LANES - SLOT), (west, lo, 0)):
+    lo, hi = half_tiles(cols)
+    groups = rows // SUB
+    for out, near, far, first in ((east, hi, lo, LANES - SLOT), (west, lo, hi, 0)):
+        for g in range(groups):
+            row = slice(SUB * g, SUB * (g + 1))
             for k in range(levels):
-                parts = [q[k, row, where] for q in (u, v, t, s)]
-                out[k, row, :] = four_slots(parts, first, lane)
-            parts = [q[row, where] for q in (sea, zonal, merid)]
-            parts.append(tally[row, where].astype(jnp.float32))
-            out[levels, row, :] = four_slots(parts, first, lane)
+                parts = [q[k, row, near] for q in (u, v, t, s)]
+                out[groups * k + g] = four_slots(parts, first, lane)
+            parts = [q[row, near] for q in (sea, zonal, merid)]
+            parts.append(tally[row, near].astype(jnp.float32))
+            out[groups * levels + g] = four_slots(parts, first, lane)
+        base, row = groups * (levels + 1), slice(rows - SUB, rows)
+        edges = []
+        for k, q in enumerate((u, v, t, s)):
+            tile = jnp.swapaxes(q[:, row, near], 0, 1)
+            for j in range(DEEP):
+                out[base + k * DEEP + j] = tile[SUB - DEEP + j]
+            edges.append(jnp.swapaxes(q[:, row, far], 0, 1))
+        for j in range(DEEP):
+            parts = [edge[SUB - DEEP + j] for edge in edges]
+            out[base + FIELDS * DEEP + j] = four_slots(parts, first, lane)
+        out[base + (FIELDS + 1) * DEEP] = tally[row, near].astype(jnp.float32)
+        out[base + (FIELDS + 1) * DEEP + 1] = tally[row, far].astype(jnp.float32)
 
 
 def halo_tile(from_east, from_west, k, lane):
@@ -87,20 +101,20 @@
     flat,
     msg_a,
     msg_b,
-    msg_c,
 ):
     levels, rows, cols = u.shape
     lane = lane_of((SUB, LANES))
     own, halo = slice(0, cols), slice(cols, cols + LANES)
-    for g in range(rows // SUB):
+    groups = rows // SUB
+    for g in range(groups):
         row = slice(SUB * g, SUB * (g + 1))
         for k, q in enumerate((u, v, t, s)):
             fields[k, row, :, own] = jnp.swapaxes(q[:, row, :], 0, 1)
-            tiles = [halo_tile(from_east[i, row, :], from_west[i, row, :], k, lane) for i in range(levels)]
+            tiles = [halo_tile(from_east[groups * i + g], from_west[groups * i + g], k, lane) for i in range(levels)]
             fields[k, row, :, halo] = jnp.swapaxes(jnp.stack(tiles), 0, 1)
         for k, q in enumerate((sea, zonal, merid, tally)):
             flat[k, row, own] = q[row, :].astype(jnp.float32)
-            flat[k, row, halo] = halo_tile(from_east[levels, row, :], from_west[levels, row, :], k, lane)
+            flat[k, row, halo] = halo_tile(from_east[groups * levels + g], from_west[groups * levels + g], k, lane)
     even = lax.rem(lax.axis_index("lat"), 2) == 0
 
     def fill(msg, first):
@@ -115,25 +129,40 @@
         fill(msg_a, rows - DEEP)
         fill(msg_b, 0)
 
+    top = lax.axis_index("lat") == top_lat
+
     @pl.when(jnp.logical_not(even))
     def _():
         fill(msg_a, 0)
+
+    @pl.when(jnp.logical_not(even) & jnp.logical_not(top))
+    def _():
         fill(msg_b, rows - DEEP)
 
-    @pl.when(lax.axis_index("lat") == top_lat)
-    def _():
-        west, _ = fold_offset(seam, cols)
+    @pl.when(top)
+    def _():
+        west, rest = fold_offset(seam, cols)
         first = jnp.where(west, LANES - SLOT, 0)
-        for q in range(DEEP):
-            edges = []
-            for k in range(FIELDS):
-                low, high = (fields[k, rows - DEEP + q, :, at] for at in half_tiles(cols))
-                msg_c[k * DEEP + q] = jnp.where(west, high, low)
-                edges.append(jnp.where(west, low, high))
-            msg_c[FIELDS * DEEP + q] = four_slots(edges, first, lane)
-        low, high = (msg_b[FIELDS * DEEP, :, at] for at in half_tiles(cols))
-        msg_c[(FIELDS + 1) * DEEP] = jnp.where(west, high, low)
-        msg_c[(FIELDS + 1) * DEEP + 1] = jnp.where(west, low, high)
+        base = groups * (levels + 1)
+        tiles = [slice(LANES * i, LANES * (i + 1)) for i in range(cols // LANES + 1)]
+
+        def beside(plane):
+            return jnp.where(west, from_west[base + plane], from_east[base + plane])
+
+        edges = [beside(FIELDS * DEEP + q) for q in range(DEEP)]
+        for k in range(FIELDS):
+            for q in range(DEEP):
+                parts = [fields[k, rows - DEEP + q, :, at] for at in tiles]
+                edge = own_slot(edges[q], k, first)
+                line = facing_line(west, parts[:-1], parts[-1], beside(k * DEEP + q), edge)
+                for at, ghost in zip(tiles, across_fold(line, rest, lane)):
+                    msg_b[k * DEEP + DEEP - 1 - q, :, at] = -ghost if k < 2 else ghost
+        half = (FIELDS + 1) * DEEP
+        parts = [flat[3, rows - SUB : rows, at] for at in tiles]
+        line = facing_line(west, parts[:-1], parts[-1], beside(half), beside(half + 1))
+        for at, ghost in zip(tiles, across_fold(line, rest, lane)):
+            msg_b[FIELDS * DEEP, :, at] = jnp.zeros_like(ghost)
+            msg_b[FIELDS * DEEP, 0:1, at] = ghost[SUB - 1 : SUB, :]
 
 
 def fold_offset(seam, cols):
@@ -219,12 +248,10 @@
 
 def force_kernel(
     sizes,
-    seam,
     fields,
     flat,
     got_a,
     got_b,
-    got_c,
     base_u,
     base_v,
     six,
@@ -242,8 +269,6 @@
     width = cols + LANES
     lat = lax.axis_index("lat")
     even = lax.rem(lat, 2) == 0
-    top = lat == lat_size - 1
-    lane = lane_of((SUB, LANES))
     planes = FIELDS * DEEP
 
     @pl.when(even)
@@ -254,30 +279,11 @@
     @pl.when(jnp.logical_not(even))
     def _():
         south[...] = got_a[...]
-
-    @pl.when(jnp.logical_not(even) & jnp.logical_not(top))
-    def _():
         north[...] = got_b[...]
 
-    @pl.when(top)
-    def _():
-        west, rest = fold_offset(seam, cols)
-        first = jnp.where(west, LANES - SLOT, 0)
-        tiles = [slice(LANES * i, LANES * (i + 1)) for i in range(width // LANES)]
-
-        def ghosts(plane, half, half_edge):
-            parts = [got_b[plane, :, at] for at in tiles]
-            line = facing_line(west, parts[:-1], parts[-1], half, half_edge)
-            return across_fold(line, rest, lane)
-
-        for k in range(FIELDS):
-            for q in range(DEEP):
-                plane = k * DEEP + q
-                edge = own_slot(got_c[planes + q], k, first)
-                for at, ghost in zip(tiles, ghosts(plane, got_c[plane], edge)):
-                    north[k * DEEP + DEEP - 1 - q, :, at] = -ghost if k < 2 else ghost
-        for at, ghost in zip(tiles, ghosts(planes, got_c[planes + DEEP], got_c[planes + DEEP + 1])):
-            north[planes, 0:1, at] = ghost[DEEP - 1 : DEEP, :]
+    @pl.when(lat == 0)
+    def _():
+        south[...] = jnp.zeros_like(south)
 
     level = lax.broadcasted_iota(jnp.int32, (SUB, width), 0)
     level_real = level.astype(jnp.float32)
@@ -474,6 +480,12 @@
     @pl.when(pair_even)
     def _():
         space[:, below, :] = got_2[0][...] if got_2 else jnp.zeros_like(got_1)
+        if got_2:
+
+            @pl.when(pair == 0)
+            def _():
+                space[:, below, :] = jnp.zeros_like(got_1)
+
         space[:, above, :] = got_1[...]
 
     @pl.when(jnp.logical_not(pair_even))
@@ -562,7 +574,7 @@
     return jax.ShapeDtypeStruct(shape, jnp.float32)
 
 
-def call(kernel, outs, scratch=(), seam=False):
+def call(kernel, outs, scratch=(), seam=False, grant=GRANT):
     vmem = pl.BlockSpec(memory_space=pltpu.VMEM)
 
     def run(*args):
@@ -575,6 +587,7 @@
             in_specs=specs,
             out_specs=jax.tree.map(lambda _: vmem, outs),
             scratch_shapes=[pltpu.VMEM(shape, jnp.float32) for shape in scratch],
+            compiler_params=pltpu.CompilerParams(vmem_limit_bytes=grant),
         )(*args)
 
     return run
@@ -586,7 +599,9 @@
     width = cols + LANES
     assert levels == SUB and rows % SUB == 0 and lat_size % 4 == 0
     tile = lax.rem(lax.div(seam[0], cols) + lax.axis_index("lon"), lon_size)
-    choice = 2 * tile + (lax.rem(seam[0], cols) >= cols // 2).astype(jnp.int32)
+    west_half = (lax.rem(seam[0], cols) >= cols // 2).astype(jnp.int32)
+    choice = 2 * tile + west_half
+    facing = lax.rem(tile + west_half + lon_size - 1, lon_size)
 
     def partners(chosen):
         turn, west = divmod(chosen, 2)
@@ -596,7 +611,8 @@
         pairs = [(x * lat_size + a, x * lat_size + b) for a, b in lats for x in range(lon_size)]
         for a in fold:
             pairs += [(x * lat_size + a, (turn - x) % lon_size * lat_size + a) for x in range(lon_size)]
-        return pairs
+        busy = {a for a, _ in pairs}
+        return pairs + [(i, i) for i in range(lon_size * lat_size) if i not in busy]
 
     def send(values, pairs):
         return lax.ppermute(values, ("lon", "lat"), pairs)
@@ -612,41 +628,31 @@
     chips_2 = both((2 * c + b, 2 * c + 2 + b) for c in range(1, chips - 1, 2) for b in (0, 1))
     high, low = (lat_size - 1,), (lat_size - 2,)
 
-    message = real(levels + 1, rows, LANES)
+    message = real((levels + 1) * rows // SUB + (FIELDS + 1) * DEEP + 2, SUB, LANES)
     flat_args = (u, v, t, s, sea, zonal, merid, tally)
-    east, west = call(pack_kernel, (message, message))(*flat_args)
+    east, west = call(pack_kernel, (message, message), grant=None)(*flat_args)
     from_west = lax.ppermute(east, "lon", ring)
     from_east = lax.ppermute(west, "lon", [(b, a) for a, b in ring])
 
     deep = real(FIELDS * DEEP + 1, SUB, width)
-    fields, flat, msg_a, msg_b, msg_c = call(
+    fields, flat, msg_a, msg_b = call(
         functools.partial(widen_kernel, lat_size - 1),
         (
             real(FIELDS, rows, SUB, width),
             real(FIELDS, rows, width),
             deep,
             deep,
-            real((FIELDS + 1) * DEEP + 2, SUB, LANES),
         ),
         seam=True,
     )(seam, *flat_args, from_west, from_east)
 
-    def deep_exchange(chosen):
-        whole, half = partners(chosen)
-
-        def run(a, b, c):
-            return (
-                send(a, moves(inside)),
-                send(b, moves(between, high, whole)),
-                send(c, moves((), high, half)),
-            )
+    def deep_exchange(turn):
+        def run(a, b):
+            return send(a, moves(inside)), send(b, moves(between, high, turn))
 
         return run
 
-    branches = range(2 * lon_size)
-    got_a, got_b, got_c = lax.switch(
-        choice, [deep_exchange(i) for i in branches], msg_a, msg_b, msg_c
-    )
+    got_a, got_b = lax.switch(facing, [deep_exchange(i) for i in range(lon_size)], msg_a, msg_b)
 
     base = real(rows, SUB, cols)
     tracer = real(levels, rows, cols)
@@ -655,8 +661,7 @@
         functools.partial(force_kernel, (rows, lat_size)),
         (base, base, real(6, rows, width), deep, deep, real(rows + 1, SUB, width), wide, wide),
         scratch=((rows + 2, SUB, width), (2, rows + 1, SUB, width), (rows + 2, SUB, width)),
-        seam=True,
-    )(seam, fields, flat, got_a, got_b, got_c)
+    )(fields, flat, got_a, got_b)
 
     got_pair = send(six, moves(inside))
     count = six.shape[0]
@@ -691,7 +696,7 @@
 
     received, (tracer_t, tracer_s) = lax.switch(
         choice,
-        [strip_exchange(i) for i in branches],
+        [strip_exchange(i) for i in range(2 * lon_size)],
         messages,
         (fields, flat, south, north, speed_n, speed_e, rises),
     )

time: 55.7 us -> 51.3 us (0.921); the launches traced: 56.6 us -> 50.6 us
  local copies, waits for them, and re-layouts: 3.09 us -> 0.56 us
  Pallas kernels: 23.3 us -> 21.1 us
  waiting for transfers between devices: 6.63 us -> 5.39 us
    unnamed x8 -> x18, local copies, waits for them, and re-layouts: 2.57 us -> 0.04 us
    pallas_call x6, Pallas kernels: 23.3 us -> 21.1 us  [run(): pl.pallas_call(kernel, out_shape=outs, in_specs=specs, out_specs=jax.tree...]
    ppermute x9 -> x8, waiting for transfers between devices: 6.63 us -> 4.47 us  [send(): return lax.ppermute(values, ('lon', 'lat'), pairs)]
    ppermute x1, waiting for transfers between devices: 0.01 us -> 0.92 us  [on_device(): from_west = lax.ppermute(east, 'lon', ring)]
    ppermute x9 -> x8, starting transfers between devices: 16.2 us -> 16.3 us  [send(): return lax.ppermute(values, ('lon', 'lat'), pairs)]
  transfers between devices with their start and end apart: 11 -> 10, of which waited for: 2 -> 3; matrix products, arithmetic and copies ran while one was open for 1% -> 1% of each run, Pallas kernels for 8% -> 9%
where the time goes in v3:
time: 51.3 us; the launch traced here: 50.6 us
  Pallas kernels  21.1 us (41%)
  starting transfers between devices  20.7 us (40%)
  waiting for transfers between devices  5.39 us (11%)
  between operations  2.77 us (5%)
  local copies, waits for them, and re-layouts  0.56 us (1%)
    pallas_call x6, Pallas kernels, run(): pl.pallas_call(kernel, out_shape=outs, in_specs=specs, out_specs=jax.tree...  21.1 us
    ppermute x8, starting transfers between devices, send(): return lax.ppermute(values, ('lon', 'lat'), pairs)  16.3 us
    ppermute x8, waiting for transfers between devices, send(): return lax.ppermute(values, ('lon', 'lat'), pairs)  4.47 us
    ppermute x1, starting transfers between devices, on_device(): from_east = lax.ppermute(west, 'lon', [(b, a) for a, b in ring])  3.1 us
    ppermute x1, starting transfers between devices, on_device(): from_west = lax.ppermute(east, 'lon', ring)  1.24 us
  transfers between devices with their start and end apart: 10, of which 3 were waited for; matrix products, arithmetic and copies ran while one was open for 1% of the time, Pallas kernels for 9%

profile of v3, /device:TPU:3, one launch (start us, length us, event | category | flops | bytes accessed | tf_op | source)
XLA Modules:
  0.0 50.6 jit_solution(13118390327830371490)
XLA Ops:
  0.7 2.0 %shard_map.144 = (f32[35,8,128]{2,1,0:T(8,128)}, f32[35,8,128]{2,1,0:T(8,128)}) custom-call(f32[8,16,256]{2,1,0:T(8,128)} %u.3, f32[8,16,256]{2,1,0:T(8,128)} %v.3, f32[8,16,256]{2,1,0:T(8,128)} %t.3, f32[8,16,256]{2,1,0:T(8,128)} %s.3, f32[16,256]{1,0:T(8,128)} %sea.3, f32[16,256]{1,0:T(8,128)} %zonal.3, f32[16,256]{1,0:T(8,128)} %merid.3, s32[16,256]{1,0:T(8,128)} %tally.3), custom_call_target="tpu_custom_call" | custom-call | tf_op jit(solution)/shard_map/pallas_call | solution.py:584
  2.7 1.2 %collective-permute-start.96 = (f32[35,8,128]{2,1,0:T(8,128)}, f32[35,8,128]{2,1,0:T(8,128)S(1)}, u32[]{:S(2)}, u32[]{:S(2)}) collective-permute-start(f32[35,8,128]{2,1,0:T(8,128)} %get-tuple-element.696), channel_id=1, source_target_pairs={{0,4},{4,8},{8,12},{12,16},{16,20},{20,24},{24,28},{28,0},{1,5},{5... | collective-permute-start | bytes 430088 | tf_op jit(solution)/shard_map/ppermute | solution.py:634
  4.0 3.1 %collective-permute-start.97 = (f32[35,8,128]{2,1,0:T(8,128)}, f32[35,8,128]{2,1,0:T(8,128)S(1)}, u32[]{:S(2)}, u32[]{:S(2)}) collective-permute-start(f32[35,8,128]{2,1,0:T(8,128)} %get-tuple-element.697), channel_id=1, source_target_pairs={{4,0},{8,4},{12,8},{16,12},{20,16},{24,20},{28,24},{0,28},{5,1},{9... | collective-permute-start | bytes 430088 | tf_op jit(solution)/shard_map/ppermute | solution.py:635
  7.1 0.5 %slice.4 = s32[1]{0:T(128)} slice(s32[256]{0:T(256)S(1)} %copy-done.8), slice={[0:1]} | slice | bytes 8 | tf_op jit(solution)/shard_map/slice | solution.py:601
  8.9 0.0 copy-start.6
  9.6 0.0 copy-start.4
  9.6 0.0 copy-start.5
  9.6 0.9 %collective-permute-done.96.from_west = f32[35,8,128]{2,1,0:T(8,128)S(1)} collective-permute-done((f32[35,8,128]{2,1,0:T(8,128)}, f32[35,8,128]{2,1,0:T(8,128)S(1)}, u32[]{:S(2)}, u32[]{:S(2)}) %collective-permute-start.96) | collective-permute-done | bytes 143392 | tf_op jit(solution)/shard_map/ppermute | solution.py:634
  10.5 0.0 collective-permute-done.97.from_east
  10.6 1.2 %shard_map.145 = (f32[4,16,8,384]{3,2,1,0:T(8,128)S(1)}, f32[4,16,384]{2,1,0:T(8,128)S(1)}, f32[13,8,384]{2,1,0:T(8,128)S(1)}, f32[13,8,384]{2,1,0:T(8,128)S(1)}) custom-call(s32[256]{0:T(256)S(1)} %copy-done.8, f32[8,16,256]{2,1,0:T(8,128)S(1)} %copy-done, f32[8,16,256]{2,1,0:T(8,128)S(1)} %copy-done.1, f32[8,16,256]{2,1,0:T(8,128)S(1)} %copy-done.2, ...), custom_call_target="tpu_custom_call" | custom-call | tf_op jit(solution)/shard_map/pallas_call | solution.py:584
  11.8 9.0 %conditional.2 = (f32[13,8,384]{2,1,0:T(8,128)}, f32[13,8,384]{2,1,0:T(8,128)}) conditional(s32[]{:T(128)} %clamp.6, (f32[13,8,384]{2,1,0:T(8,128)S(1)}, f32[13,8,384]{2,1,0:T(8,128)S(1)}) %tuple.104, (f32[13,8,384]{2,1,0:T(8,128)S(1)}, f32[13,8,384]{2,1,0:T(8,128)S(1)}) %tuple.104, (f32[13,8,384]{2,1,0:T(8,128)S(1)}, ...), branch_computations={%region_0.0_spmd, %region_1.0_spmd, %region_2.0_spmd, %region_3.0_... | conditional | bytes 1278048 | solution.py:655
  11.8 2.6 %collective-permute-start.4 = (f32[13,8,384]{2,1,0:T(8,128)S(1)}, f32[13,8,384]{2,1,0:T(8,128)}, u32[]{:S(2)}, u32[]{:S(2)}) collective-permute-start(f32[13,8,384]{2,1,0:T(8,128)S(1)} %get-tuple-element.420), channel_id=1, source_target_pairs={{0,1},{4,5},{8,9},{12,13},{16,17},{20,21},{24,25},{28,29},{1,0},{5... | collective-permute-start | bytes 479240 | tf_op jit(solution)/shard_map/cond/branch_2_fun/ppermute | solution.py:618
  14.4 2.9 %collective-permute-start.5 = (f32[13,8,384]{2,1,0:T(8,128)S(1)}, f32[13,8,384]{2,1,0:T(8,128)}, u32[]{:S(2)}, u32[]{:S(2)}) collective-permute-start(f32[13,8,384]{2,1,0:T(8,128)S(1)} %get-tuple-element.421), channel_id=1, source_target_pairs={{1,2},{5,6},{9,10},{13,14},{17,18},{21,22},{25,26},{29,30},{2,1},{... | collective-permute-start | bytes 479240 | tf_op jit(solution)/shard_map/cond/branch_2_fun/ppermute | solution.py:618
  17.3 0.0 collective-permute-done.4
  17.3 3.4 %collective-permute-done.5 = f32[13,8,384]{2,1,0:T(8,128)} collective-permute-done((f32[13,8,384]{2,1,0:T(8,128)S(1)}, f32[13,8,384]{2,1,0:T(8,128)}, u32[]{:S(2)}, u32[]{:S(2)}) %collective-permute-start.5) | collective-permute-done | bytes 159776 | tf_op jit(solution)/shard_map/cond/branch_2_fun/ppermute | solution.py:618
  20.7 5.7 %shard_map.146 = (f32[16,8,256]{2,1,0:T(8,128)S(1)}, f32[16,8,256]{2,1,0:T(8,128)S(1)}, f32[6,16,384]{2,1,0:T(8,128)S(1)}, f32[13,8,384]{2,1,0:T(8,128)S(1)}, f3...) custom-call(f32[4,16,8,384]{3,2,1,0:T(8,128)S(1)} %get-tuple-element, ...), custom_call_target="tpu_custom_call" | custom-call | tf_op jit(solution)/shard_map/pallas_call | solution.py:584
  26.4 0.5 collective-permute-start.98
  26.9 1.0 %collective-permute-done.98.got_a = f32[6,16,384]{2,1,0:T(8,128)S(1)} collective-permute-done((f32[6,16,384]{2,1,0:T(8,128)S(1)}, f32[6,16,384]{2,1,0:T(8,128)S(1)}, u32[]{:S(2)}, u32[]{:S(2)}) %collective-permute-start.98) | collective-permute-done | bytes 147488 | tf_op jit(solution)/shard_map/ppermute | solution.py:618
  27.9 0.7 %shard_map.147 = (f32[6,24,384]{2,1,0:T(8,128)S(1)}, f32[14,24,128]{2,1,0:T(8,128)S(1)}, f32[14,8,128]{2,1,0:T(8,128)S(1)}, f32[8,24,128]{2,1,0:T(8,128)S(1)}, f32[8,8,128]{2,1,0:T(8,128)S(1)}) custom-call(s32[256]{0:T(256)S(1)} %copy-done.8, f32[6,16,384]{2,1,0:T(8,128)S(1)} %get-tuple-element.704.six, f32[6,16,384]{2,1,0:T(8,128)S(1)} %collective-permute-done.98.got_a), custom_call_target="tpu_custom_call" | custom-call | tf_op jit(solution)/shard_map/pallas_call | solution.py:584
  28.6 15.2 %conditional.3 = (f32[6,24,384]{2,1,0:T(8,128)}, f32[14,24,128]{2,1,0:T(8,128)}, f32[14,8,128]{2,1,0:T(8,128)}, f32[8,24,128]{2,1,0:T(8,128)}, f32[8,8,128]{2,1,...) conditional(s32[]{:T(128)} %clamp.7, (f32[6,24,384]{2,1,0:T(8,128)S(1)}, ...), branch_computations={%region_8.0_spmd, %region_9.0_spmd, %region_10.0_spmd, %region_11.... | conditional | bytes 2326784 | solution.py:697
  28.7 0.5 %collective-permute-start.46 = (f32[6,24,384]{2,1,0:T(8,128)S(1)}, f32[6,24,384]{2,1,0:T(8,128)}, u32[]{:S(2)}, u32[]{:S(2)}) collective-permute-start(f32[6,24,384]{2,1,0:T(8,128)S(1)} %get-tuple-element.516), channel_id=1, source_target_pairs={{0,2},{4,6},{8,10},{12,14},{16,18},{20,22},{24,26},{28,30},{2,0},{... | collective-permute-start | bytes 663560 | tf_op jit(solution)/shard_map/cond/branch_6_fun/ppermute | solution.py:618
  29.2 2.9 %collective-permute-start.47 = (f32[14,24,128]{2,1,0:T(8,128)S(1)}, f32[14,24,128]{2,1,0:T(8,128)}, u32[]{:S(2)}, u32[]{:S(2)}) collective-permute-start(f32[14,24,128]{2,1,0:T(8,128)S(1)} %get-tuple-element.517), channel_id=1, source_target_pairs={{3,11},{7,7},{11,3},{15,31},{19,27},{23,23},{27,19},{31,15},{0,0},... | collective-permute-start | bytes 516104 | tf_op jit(solution)/shard_map/cond/branch_6_fun/ppermute | solution.py:618
  32.1 4.5 %collective-permute-start.49 = (f32[8,24,128]{2,1,0:T(8,128)S(1)}, f32[8,24,128]{2,1,0:T(8,128)}, u32[]{:S(2)}, u32[]{:S(2)}) collective-permute-start(f32[8,24,128]{2,1,0:T(8,128)S(1)} %get-tuple-element.519), channel_id=1, source_target_pairs={{3,15},{7,11},{11,7},{15,3},{19,31},{23,27},{27,23},{31,19},{0,0},... | collective-permute-start | bytes 294920 | tf_op jit(solution)/shard_map/cond/branch_6_fun/ppermute | solution.py:618
  36.6 1.3 %collective-permute-start.48 = (f32[14,8,128]{2,1,0:T(8,128)S(1)}, f32[14,8,128]{2,1,0:T(8,128)}, u32[]{:S(2)}, u32[]{:S(2)}) collective-permute-start(f32[14,8,128]{2,1,0:T(8,128)S(1)} %get-tuple-element.518), channel_id=1, source_target_pairs={{2,10},{6,6},{10,2},{14,30},{18,26},{22,22},{26,18},{30,14},{0,0},... | collective-permute-start | bytes 172040 | tf_op jit(solution)/shard_map/cond/branch_6_fun/ppermute | solution.py:618
  37.8 1.2 %collective-permute-start.50 = (f32[8,8,128]{2,1,0:T(8,128)S(1)}, f32[8,8,128]{2,1,0:T(8,128)}, u32[]{:S(2)}, u32[]{:S(2)}) collective-permute-start(f32[8,8,128]{2,1,0:T(8,128)S(1)} %get-tuple-element.520), channel_id=1, source_target_pairs={{2,14},{6,10},{10,6},{14,2},{18,30},{22,26},{26,22},{30,18},{0,0},... | collective-permute-start | bytes 98312 | tf_op jit(solution)/shard_map/cond/branch_6_fun/ppermute | solution.py:618
  39.1 4.6 %branch_6_fun.1 = (f32[8,16,256]{2,1,0:T(8,128)}, f32[8,16,256]{2,1,0:T(8,128)}) custom-call(f32[4,16,8,384]{3,2,1,0:T(8,128)S(1)} %get-tuple-element.521.fields, f32[4,16,384]{2,1,0:T(8,128)S(1)} %get-tuple-element.522.flat, f32[13,8,384]{2,1,0:T(8,128)S(1)} %get-tuple-element.523.south, f32[13,8,384]{2,1,0:T(8,128)S(1)} %get-tuple-element.524.north, ...), custom_call_target="tpu_custom_call" | custom-call | tf_op jit(solution)/shard_map/cond/branch_6_fun/pallas_call | solution.py:584
  43.7 0.0 collective-permute-done.50
  43.7 0.0 collective-permute-done.48
  43.7 0.0 collective-permute-done.49
  43.7 0.0 collective-permute-done.47
  43.7 0.0 collective-permute-done.46
  43.8 6.8 %shard_map.148 = (f32[8,16,256]{2,1,0:T(8,128)}, f32[8,16,256]{2,1,0:T(8,128)}, f32[16,256]{1,0:T(8,128)}, f32[16,256]{1,0:T(8,128)}, f32[16,256]{1,0:T(8,128)}) custom-call(s32[256]{0:T(256)S(1)} %copy-done.8, f32[6,16,384]{2,1,0:T(8,128)S(1)} %get-tuple-element.704.six, f32[6,16,384]{2,1,0:T(8,128)S(1)} %collective-permute-done.98.got_a, ...), custom_call_target="tpu_custom_call" | custom-call | tf_op jit(solution)/shard_map/pallas_call | solution.py:584
  (15 shorter events, 0.0 us)
Async XLA Ops:
  0.6 6.4 %copy-start.8 = (s32[256]{0:T(256)S(1)}, s32[256]{0:T(256)}, u32[]{:S(2)}) copy-start(s32[256]{0:T(256)} %seam.5) | copy-start | bytes 3076
  0.6 9.9 %copy-start = (f32[8,16,256]{2,1,0:T(8,128)S(1)}, f32[8,16,256]{2,1,0:T(8,128)}, u32[]{:S(2)}) copy-start(f32[8,16,256]{2,1,0:T(8,128)} %u.3) | copy-start | bytes 393220
  0.7 9.9 %copy-start.1 = (f32[8,16,256]{2,1,0:T(8,128)S(1)}, f32[8,16,256]{2,1,0:T(8,128)}, u32[]{:S(2)}) copy-start(f32[8,16,256]{2,1,0:T(8,128)} %v.3) | copy-start | bytes 393220
  0.7 9.9 %copy-start.2 = (f32[8,16,256]{2,1,0:T(8,128)S(1)}, f32[8,16,256]{2,1,0:T(8,128)}, u32[]{:S(2)}) copy-start(f32[8,16,256]{2,1,0:T(8,128)} %t.3) | copy-start | bytes 393220
  0.7 9.9 %copy-start.3 = (f32[8,16,256]{2,1,0:T(8,128)S(1)}, f32[8,16,256]{2,1,0:T(8,128)}, u32[]{:S(2)}) copy-start(f32[8,16,256]{2,1,0:T(8,128)} %s.3) | copy-start | bytes 393220
  2.7 7.8 %copy-start.7 = (s32[16,256]{1,0:T(8,128)S(1)}, s32[16,256]{1,0:T(8,128)}, u32[]{:S(2)}) copy-start(s32[16,256]{1,0:T(8,128)} %tally.3) | copy-start | bytes 49156
  2.7 7.8 %collective-permute-start.96 = (f32[35,8,128]{2,1,0:T(8,128)}, f32[35,8,128]{2,1,0:T(8,128)S(1)}, u32[]{:S(2)}, u32[]{:S(2)}) collective-permute-start(f32[35,8,128]{2,1,0:T(8,128)} %get-tuple-element.696), channel_id=1, source_target_pairs={{0,4},{4,8},{8,12},{12,16},{16,20},{20,24},{24,28},{28,0},{1,5},{5... | collective-permute-start | bytes 430088 | tf_op jit(solution)/shard_map/ppermute | solution.py:634
  4.0 6.5 %collective-permute-start.97 = (f32[35,8,128]{2,1,0:T(8,128)}, f32[35,8,128]{2,1,0:T(8,128)S(1)}, u32[]{:S(2)}, u32[]{:S(2)}) collective-permute-start(f32[35,8,128]{2,1,0:T(8,128)} %get-tuple-element.697), channel_id=1, source_target_pairs={{4,0},{8,4},{12,8},{16,12},{20,16},{24,20},{28,24},{0,28},{5,1},{9... | collective-permute-start | bytes 430088 | tf_op jit(solution)/shard_map/ppermute | solution.py:635
  8.9 1.7 %copy-start.6 = (f32[16,256]{1,0:T(8,128)S(1)}, f32[16,256]{1,0:T(8,128)}, u32[]{:S(2)}) copy-start(f32[16,256]{1,0:T(8,128)} %merid.3) | copy-start | bytes 49156
  9.6 1.0 %copy-start.4 = (f32[16,256]{1,0:T(8,128)S(1)}, f32[16,256]{1,0:T(8,128)}, u32[]{:S(2)}) copy-start(f32[16,256]{1,0:T(8,128)} %sea.3) | copy-start | bytes 49156
  9.6 1.0 %copy-start.5 = (f32[16,256]{1,0:T(8,128)S(1)}, f32[16,256]{1,0:T(8,128)}, u32[]{:S(2)}) copy-start(f32[16,256]{1,0:T(8,128)} %zonal.3) | copy-start | bytes 49156
  11.8 5.5 %collective-permute-start.4 = (f32[13,8,384]{2,1,0:T(8,128)S(1)}, f32[13,8,384]{2,1,0:T(8,128)}, u32[]{:S(2)}, u32[]{:S(2)}) collective-permute-start(f32[13,8,384]{2,1,0:T(8,128)S(1)} %get-tuple-element.420), channel_id=1, source_target_pairs={{0,1},{4,5},{8,9},{12,13},{16,17},{20,21},{24,25},{28,29},{1,0},{5... | collective-permute-start | bytes 479240 | tf_op jit(solution)/shard_map/cond/branch_2_fun/ppermute | solution.py:618
  14.4 6.3 %collective-permute-start.5 = (f32[13,8,384]{2,1,0:T(8,128)S(1)}, f32[13,8,384]{2,1,0:T(8,128)}, u32[]{:S(2)}, u32[]{:S(2)}) collective-permute-start(f32[13,8,384]{2,1,0:T(8,128)S(1)} %get-tuple-element.421), channel_id=1, source_target_pairs={{1,2},{5,6},{9,10},{13,14},{17,18},{21,22},{25,26},{29,30},{2,1},{... | collective-permute-start | bytes 479240 | tf_op jit(solution)/shard_map/cond/branch_2_fun/ppermute | solution.py:618
  26.4 1.5 %collective-permute-start.98 = (f32[6,16,384]{2,1,0:T(8,128)S(1)}, f32[6,16,384]{2,1,0:T(8,128)S(1)}, u32[]{:S(2)}, u32[]{:S(2)}) collective-permute-start(f32[6,16,384]{2,1,0:T(8,128)S(1)} %get-tuple-element.704.six), channel_id=1, source_target_pairs={{0,1},{4,5},{8,9},{12,13},{16,17},{20,21},{24,25},{28,29},{1,0},{5... | collective-permute-start | bytes 442376 | tf_op jit(solution)/shard_map/ppermute | solution.py:618
  28.7 15.1 %collective-permute-start.46 = (f32[6,24,384]{2,1,0:T(8,128)S(1)}, f32[6,24,384]{2,1,0:T(8,128)}, u32[]{:S(2)}, u32[]{:S(2)}) collective-permute-start(f32[6,24,384]{2,1,0:T(8,128)S(1)} %get-tuple-element.516), channel_id=1, source_target_pairs={{0,2},{4,6},{8,10},{12,14},{16,18},{20,22},{24,26},{28,30},{2,0},{... | collective-permute-start | bytes 663560 | tf_op jit(solution)/shard_map/cond/branch_6_fun/ppermute | solution.py:618
  29.2 14.5 %collective-permute-start.47 = (f32[14,24,128]{2,1,0:T(8,128)S(1)}, f32[14,24,128]{2,1,0:T(8,128)}, u32[]{:S(2)}, u32[]{:S(2)}) collective-permute-start(f32[14,24,128]{2,1,0:T(8,128)S(1)} %get-tuple-element.517), channel_id=1, source_target_pairs={{3,11},{7,7},{11,3},{15,31},{19,27},{23,23},{27,19},{31,15},{0,0},... | collective-permute-start | bytes 516104 | tf_op jit(solution)/shard_map/cond/branch_6_fun/ppermute | solution.py:618
  32.1 11.7 %collective-permute-start.49 = (f32[8,24,128]{2,1,0:T(8,128)S(1)}, f32[8,24,128]{2,1,0:T(8,128)}, u32[]{:S(2)}, u32[]{:S(2)}) collective-permute-start(f32[8,24,128]{2,1,0:T(8,128)S(1)} %get-tuple-element.519), channel_id=1, source_target_pairs={{3,15},{7,11},{11,7},{15,3},{19,31},{23,27},{27,23},{31,19},{0,0},... | collective-permute-start | bytes 294920 | tf_op jit(solution)/shard_map/cond/branch_6_fun/ppermute | solution.py:618
  36.6 7.2 %collective-permute-start.48 = (f32[14,8,128]{2,1,0:T(8,128)S(1)}, f32[14,8,128]{2,1,0:T(8,128)}, u32[]{:S(2)}, u32[]{:S(2)}) collective-permute-start(f32[14,8,128]{2,1,0:T(8,128)S(1)} %get-tuple-element.518), channel_id=1, source_target_pairs={{2,10},{6,6},{10,2},{14,30},{18,26},{22,22},{26,18},{30,14},{0,0},... | collective-permute-start | bytes 172040 | tf_op jit(solution)/shard_map/cond/branch_6_fun/ppermute | solution.py:618
  37.8 5.9 %collective-permute-start.50 = (f32[8,8,128]{2,1,0:T(8,128)S(1)}, f32[8,8,128]{2,1,0:T(8,128)}, u32[]{:S(2)}, u32[]{:S(2)}) collective-permute-start(f32[8,8,128]{2,1,0:T(8,128)S(1)} %get-tuple-element.520), channel_id=1, source_target_pairs={{2,14},{6,10},{10,6},{14,2},{18,30},{22,26},{26,22},{30,18},{0,0},... | collective-permute-start | bytes 98312 | tf_op jit(solution)/shard_map/cond/branch_6_fun/ppermute | solution.py:618
